TPU v7x, 32 devices: a whole 2x2x4 slice. The times are simulated.
32 devices in a mesh: dom: 8 (over z, y), rows: 4 (over x, core).
Axes of the slice: x: 2, y: 2, z: 4, core: 2. Of those that a mesh axis runs over, the one named last changes fastest.
Arguments:
- fields: float32 [8, 3, 128, 4096], P('dom', None, 'rows'), may hold values from -6 to 6
- depth: float32 [128, 4096], P('rows'), may hold values from 1.5 to 6
- obs_index: int32 [256], replicated, may hold values from 0 to 524287, as said below
- obs_value: float32 [256], replicated, may hold values from -6 to 6
- obs_var: float32 [256], replicated, may hold values from 0.5 to 5
- parent_lookup: int32 [8], replicated, may hold values from 0 to 7, as said below
Outputs:
- log_weights: float32 [8], P('dom')
- posterior_members: float32 [8, 3, 128, 4096], P('dom', None, 'rows')
Inputs may be any that keep to these rules, and one draw needn't show every extreme that they name: `parent_lookup`: every value is the index of a particle; 0 and 7 each appear; values may repeat. `obs_index`: indices of grid cells, possibly repeated; the first and last cell each appear.
All inputs are finite; a program needn't handle non-finite values.
Results may differ from a plain program's by a relative error of at most 0.00003.
Values sent between devices are 32-bit elements; how exact they have to be, the bound alone decides.
No kernel may reach another device: no remote copies, remote signals or barrier semaphores. Data moves between devices by JAX's collectives and lax.ppermute only.
A program may use at most 64 MiB of HBM per device.

v0:
```python
import jax
import jax.numpy as jnp
from jax import lax
from jax.experimental import pallas as pl
from jax.experimental.pallas import tpu as pltpu
from jax.sharding import PartitionSpec as P

STEPS = 4
HALO = 2 * STEPS
LANES = 128
VMEM_BYTES = 48 * 2**20
ROUTED_HALF = 4

time_step = 0.5
coriolis = 0.2

in_vmem = pl.BlockSpec(memory_space=pltpu.VMEM)
in_smem = pl.BlockSpec(memory_space=pltpu.SMEM)
in_hbm = pl.BlockSpec(memory_space=pltpu.HBM)


def model_steps(h_ref, u_ref, v_ref, d_ref, top_open=None, bottom_open=None):
    n_rows, n_cols = h_ref.shape
    h_ref[...] = h_ref[...] * (0.5 * time_step)
    d_ref[...] = d_ref[...] * (0.25 * time_step * time_step)

    def cols(a):
        return pltpu.roll(a, n_cols - 1, 1) - pltpu.roll(a, 1, 1)

    def rows(a):
        return pltpu.roll(a, n_rows - 1, 0) - pltpu.roll(a, 1, 0)

    def step(_, carry):
        u = u_ref[...]
        v = v_ref[...]
        d = d_ref[...]
        h = h_ref[...] - (cols(d * u) + rows(d * v))
        if top_open is not None:
            h = jnp.concatenate(
                [h[:HALO] * top_open, h[HALO : n_rows - HALO], h[n_rows - HALO :] * bottom_open], axis=0
            )
        h_ref[...] = h
        u = u - cols(h) + (time_step * coriolis) * v
        u_ref[...] = u
        v_ref[...] = v - rows(h) - (time_step * coriolis) * u
        return carry

    lax.fori_loop(0, STEPS, step, 0)
    h_ref[...] = h_ref[...] * (2.0 / time_step)


def store_pieces(at_ref, outs, state, rows_of):
    width = outs[0].shape[-1]
    for m, out in enumerate(outs):
        start = pl.multiple_of(jnp.bitwise_xor(at_ref[0], m) * width, LANES)
        for k, ref in enumerate(state[:3]):
            out[k] = rows_of(ref, pl.ds(start, width))


def inner_kernel(at_ref, fields_ref, depth_ref, *refs):
    outs, h_ref, state = refs[:-5], refs[-5], refs[-4:]
    n_rows = depth_ref.shape[0]
    for k in range(4):
        state[k][...] = depth_ref[...] if k == 3 else fields_ref[0, k]
    model_steps(*state)
    h_ref[...] = state[0][HALO : n_rows - HALO]
    store_pieces(at_ref, outs, state, lambda ref, at: ref[HALO : n_rows - HALO, at])


def outer_kernel(at_ref, fields_ref, depth_ref, above_ref, below_ref, *refs):
    outs, h_ref, state = refs[:-5], refs[-5], refs[-4:]
    n_rows = depth_ref.shape[0]
    for k in range(4):
        state[k][:HALO] = above_ref[k]
        state[k][HALO : HALO + n_rows] = depth_ref[...] if k == 3 else fields_ref[0, k]
        state[k][HALO + n_rows :] = below_ref[k]
    model_steps(*state, at_ref[1].astype(jnp.float32), at_ref[2].astype(jnp.float32))

    def outer_rows(ref, at):
        return jnp.concatenate([ref[HALO : 2 * HALO, at], ref[n_rows : n_rows + HALO, at]], axis=0)

    h_ref[...] = outer_rows(state[0], pl.ds(0, depth_ref.shape[1]))
    store_pieces(at_ref, outs, state, outer_rows)


def forecast(kernel, name, at, arrays, n_rows, n_cols, count, window_rows):
    shapes = [(3, n_rows, n_cols // count)] * count + [(n_rows, n_cols)]
    outs = pl.pallas_call(
        kernel,
        out_shape=[jax.ShapeDtypeStruct(shape, jnp.float32) for shape in shapes],
        in_specs=[in_smem] + [in_vmem] * len(arrays),
        out_specs=[in_vmem] * len(shapes),
        scratch_shapes=[pltpu.VMEM((window_rows, n_cols), jnp.float32)] * 4,
        compiler_params=pltpu.CompilerParams(vmem_limit_bytes=VMEM_BYTES),
        name=name,
    )(at, *arrays)
    return list(outs[:count]), outs[count]


def misfit_kernel(at_ref, index_ref, value_ref, var_ref, inner_ref, outer_ref, out_ref, total_ref):
    inner_rows, n_cols = inner_ref.shape
    n_rows = inner_rows + 2 * HALO
    base = at_ref[3] * (n_rows * n_cols)
    row_in = lax.broadcasted_iota(jnp.int32, (8, LANES), 0)
    lane_in = lax.broadcasted_iota(jnp.int32, (8, LANES), 1)

    def tile(ref, row, col):
        first_row = pl.multiple_of(jnp.bitwise_and(row, -8), 8)
        first_col = pl.multiple_of(jnp.bitwise_and(col, -LANES), LANES)
        return ref[pl.ds(first_row, 8), pl.ds(first_col, LANES)]

    def point(k, carry):
        offset = index_ref[k] - base

        @pl.when(jnp.logical_and(offset >= 0, offset < n_rows * n_cols))
        def _():
            row = lax.div(offset, n_cols)
            col = offset - row * n_cols
            inner_row = row - HALO
            is_inner = jnp.logical_and(inner_row >= 0, inner_row < inner_rows)
            outer_row = jnp.where(row < HALO, row, row - inner_rows)
            hit = (row_in == jnp.bitwise_and(row, 7)) & (lane_in == jnp.bitwise_and(col, LANES - 1))

            def add(seen):
                total_ref[...] += jnp.where(hit, (value_ref[k] - seen) ** 2 / var_ref[k], 0.0)

            @pl.when(is_inner)
            def _():
                add(tile(inner_ref, inner_row, col))

            @pl.when(jnp.logical_not(is_inner))
            def _():
                add(tile(outer_ref, outer_row, col))

        return carry

    total_ref[...] = jnp.zeros_like(total_ref)
    lax.fori_loop(0, index_ref.shape[0], point, 0, unroll=8)
    lane = lax.broadcasted_iota(jnp.int32, out_ref.shape, 1)
    out_ref[...] = jnp.where(lane == at_ref[5], -0.5 * jnp.sum(total_ref[...]), 0.0)


def misfit(at, obs_index, obs_value, obs_var, inner, outer):
    return pl.pallas_call(
        misfit_kernel,
        out_shape=jax.ShapeDtypeStruct((1, LANES), jnp.float32),
        in_specs=[in_smem] * 4 + [in_vmem] * 2,
        out_specs=in_vmem,
        scratch_shapes=[pltpu.VMEM((8, LANES), jnp.float32)],
        compiler_params=pltpu.CompilerParams(vmem_limit_bytes=VMEM_BYTES),
        name="misfit",
    )(at, obs_index, obs_value, obs_var, inner, outer)


def sum_over(x, axis):
    count = lax.axis_size(axis)
    step = 1
    while step < count:
        x = x + lax.ppermute(x, axis, [(i, i ^ step) for i in range(count)])
        step *= 2
    return x


def own_log_weight(loglik, own, particles):
    lane = lax.broadcasted_iota(jnp.int32, loglik.shape, 1)
    peak = jnp.max(jnp.where(lane < particles, loglik, -jnp.inf), axis=1, keepdims=True)
    total = jnp.sum(jnp.where(lane < particles, jnp.exp(loglik - peak), 0.0), axis=1, keepdims=True)
    return jnp.sum(jnp.where(lane == own, loglik - (peak + jnp.log(total)), 0.0))


def weigh_kernel(at_ref, loglik_ref, out_ref, *, particles):
    out_ref[0] = own_log_weight(loglik_ref[...], at_ref[5], particles)


def log_weight(at, loglik):
    particles = lax.axis_size("dom")
    return pl.pallas_call(
        lambda *refs: weigh_kernel(*refs, particles=particles),
        out_shape=jax.ShapeDtypeStruct((1,), jnp.float32),
        in_specs=[in_smem, in_vmem],
        out_specs=in_smem,
        name="weigh",
    )(at, loglik)


def place(at, pieces, spans, shape, into=None, shares=()):
    count = len(pieces)
    width = shape[-1] // count
    particles = lax.axis_size("dom")

    def kernel(at_ref, *refs):
        srcs = refs[:count]
        outs = refs[n_in : n_in + n_out]
        sems = refs[-1]
        copies = []
        for m in range(count):
            first = pl.multiple_of(jnp.bitwise_xor(at_ref[0], m) * width, LANES)
            for s, (src_row, dst_row, size) in enumerate(spans):
                copies.append(
                    pltpu.make_async_copy(
                        srcs[m].at[:, pl.ds(src_row, size), :],
                        outs[0].at[0, :, pl.ds(dst_row, size), pl.ds(first, width)],
                        sems.at[m * len(spans) + s],
                    )
                )
        for c in copies:
            c.start()
        if shares:
            loglik = sum(ref[...] for ref in refs[n_in - len(shares) : n_in])
            outs[1][0] = own_log_weight(loglik, at_ref[5], particles)
        for c in copies:
            c.wait()

    extra = [] if into is None else [into]
    n_in = count + len(extra) + len(shares)
    out_shape = [pltpu.HBM(shape, jnp.float32)] + [jax.ShapeDtypeStruct((1,), jnp.float32)] * bool(shares)
    n_out = len(out_shape)
    return pl.pallas_call(
        kernel,
        out_shape=out_shape,
        in_specs=[in_smem] + [in_vmem] * count + [in_hbm] * len(extra) + [in_vmem] * len(shares),
        out_specs=[in_hbm] + [in_smem] * bool(shares),
        scratch_shapes=[pltpu.SemaphoreType.DMA((count * len(spans),))],
        input_output_aliases={} if into is None else {count + 1: 0},
        compiler_params=pltpu.CompilerParams(vmem_limit_bytes=VMEM_BYTES),
        name="place",
    )(at, *pieces, *extra, *shares)


def prepare_kernel(at_ref, parents_ref, fields_ref, depth_ref, routes_ref, head_ref, tail_ref, sems, *, half):
    n_rows = depth_ref.shape[0]
    copies = []
    for ref, first in ((head_ref, 0), (tail_ref, n_rows - HALO)):
        rows = pl.ds(first, HALO)
        copies.append(pltpu.make_async_copy(fields_ref.at[0, :, rows], ref.at[pl.ds(0, 3)], sems.at[len(copies)]))
        copies.append(pltpu.make_async_copy(depth_ref.at[rows], ref.at[3], sems.at[len(copies)]))
    for c in copies:
        c.start()
    if half <= ROUTED_HALF:
        route(at_ref, parents_ref, routes_ref, half)
    for c in copies:
        c.wait()


def route(at_ref, parents_ref, out_ref, half):
    own = at_ref[0]
    side = at_ref[4]
    parents = [parents_ref[s] for s in range(2 * half)]

    def ranks(first):
        other = half - first
        running = jnp.int32(0)
        needed, rank = [], []
        for q in range(half):
            hit = jnp.int32(0)
            for s in range(half):
                hit = hit | jnp.where(parents[other + s] == first + q, 1, 0).astype(jnp.int32)
            needed.append(hit)
            rank.append(running)
            running = running + hit
        return needed, rank, running

    low = ranks(0)
    high = ranks(half)
    out_ref[0] = jnp.maximum(low[2], high[2])
    mine = [jnp.where(side == 0, a, b) for a, b in zip(low[0], high[0])]
    my_rank = [jnp.where(side == 0, a, b) for a, b in zip(low[1], high[1])]
    other_rank = [jnp.where(side == 0, b, a) for a, b in zip(low[1], high[1])]
    for k in range(half):
        chosen = jnp.int32(0)
        for q in range(half):
            chosen = jnp.where((mine[q] == 1) & (my_rank[q] == k), q, chosen)
        out_ref[1 + k] = jnp.bitwise_xor(chosen, own)
    for m in range(half):
        slot = jnp.bitwise_xor(own, m)
        parent = jnp.int32(0)
        for s in range(half):
            parent = jnp.where(slot == s, jnp.where(side == 0, parents[s], parents[half + s]), parent)
        local = parent - side * half
        remote = parent - (1 - side) * half
        from_rank = jnp.int32(0)
        for q in range(half):
            from_rank = jnp.where(remote == q, other_rank[q], from_rank)
        is_local = jnp.logical_and(local >= 0, local < half)
        out_ref[1 + half + m] = jnp.where(is_local, jnp.bitwise_xor(local, own), half + from_rank)


def prepare(at, parent_lookup, fields, depth, half):
    n_rows, n_cols = depth.shape
    rim = jax.ShapeDtypeStruct((4, HALO, n_cols), jnp.float32)
    return pl.pallas_call(
        lambda *refs: prepare_kernel(*refs, half=half),
        out_shape=[jax.ShapeDtypeStruct((1 + 2 * half,), jnp.int32), rim, rim],
        in_specs=[in_smem, in_smem, in_hbm, in_hbm],
        out_specs=[in_smem, in_vmem, in_vmem],
        scratch_shapes=[pltpu.SemaphoreType.DMA((4,))],
        compiler_params=pltpu.CompilerParams(vmem_limit_bytes=VMEM_BYTES),
        name="prepare",
    )(at, parent_lookup, fields, depth)


def to_mate(x, m):
    return lax.ppermute(x, "dom", [(i, i ^ m) for i in range(lax.axis_size("dom"))])


def among_mates(pieces):
    return [x if m == 0 else to_mate(x, m) for m, x in enumerate(pieces)]


def pick(routes, first, count, sources, stacks=(), stacked=False, cost=None):
    block = sources[0].shape

    def kernel(routes_ref, *refs):
        n_in = len(sources) + len(stacks)
        srcs = [(ref, None) for ref in refs[: len(sources)]]
        srcs += [(ref, k) for ref in refs[len(sources) : n_in] for k in range(ref.shape[0])]
        for m in range(count):
            which = routes_ref[first + m]
            for s, (src, k) in enumerate(srcs):

                @pl.when(which == s)
                def _(m=m, src=src, k=k):
                    value = src[...] if k is None else src[k]
                    if stacked:
                        refs[n_in][m] = value
                    else:
                        refs[n_in + m][...] = value

    shapes = [(count,) + block] if stacked else [block] * count
    return pl.pallas_call(
        kernel,
        out_shape=[jax.ShapeDtypeStruct(shape, jnp.float32) for shape in shapes],
        in_specs=[in_smem] + [in_vmem] * (len(sources) + len(stacks)),
        out_specs=[in_vmem] * len(shapes),
        compiler_params=pltpu.CompilerParams(vmem_limit_bytes=VMEM_BYTES),
        cost_estimate=cost,
        name="pick",
    )(routes, *sources, *stacks)


def chosen(held, routes, crossing, cost=None):
    return pick(routes, 1, crossing, held, stacked=True, cost=cost)[0]


def for_slots(held, got, routes):
    return pick(routes, 1 + len(held), len(held), held, [got])


def after(x, *earlier):
    return lax.optimization_barrier((x, earlier))[0]


def halo_rows(head, tail):
    count = lax.axis_size("rows")
    above = lax.ppermute(tail, "rows", [(i, i + 1) for i in range(count - 1)])
    below = lax.ppermute(head, "rows", [(i + 1, i) for i in range(count - 1)])
    return above, below


def inner_forecast(at, fields, depth, count):
    n_rows, n_cols = depth.shape
    return forecast(inner_kernel, "inner", at, (fields, depth), n_rows - 2 * HALO, n_cols, count, n_rows)


def outer_forecast(at, fields, depth, above, below, count):
    n_rows, n_cols = depth.shape
    arrays = (fields, depth, above, below)
    return forecast(outer_kernel, "outer", at, arrays, 2 * HALO, n_cols, count, n_rows + 2 * HALO)


def cycle(crossing, routes, head, tail, at, fields, depth, obs_index, obs_value, obs_var):
    half = lax.axis_size("dom") // 2
    n_rows, n_cols = depth.shape
    above, below = halo_rows(head, tail)
    inner, inner_h = inner_forecast(at, fields, depth, half)
    inner_held = among_mates(inner)
    outer, outer_h = outer_forecast(at, fields, depth, above, below, half)
    outer_held = among_mates(outer)
    inner_chosen = chosen(after(inner_held, outer), routes, crossing)
    inner_got = to_mate(inner_chosen, half)
    loglik = misfit(at, obs_index, obs_value, obs_var, inner_h, after(outer_h, inner_chosen))
    rows_first = crossing == 2
    if rows_first:
        loglik = sum_over(loglik, "rows")
    step = 1
    while step < half:
        loglik = loglik + to_mate(loglik, step)
        step *= 2
    outer_ready = after(outer_held, loglik) if rows_first else after(outer_held, loglik, inner_got)
    outer_chosen = chosen(outer_ready, routes, crossing)
    outer_got = to_mate(outer_chosen, half)
    inner_done = among_mates(for_slots(inner_held, after(inner_got, outer_chosen), routes))
    if not rows_first:
        loglik = sum_over(after(loglik, outer_chosen), "rows")
    outer_slots = for_slots(outer_held, outer_got, routes)
    outer_done = among_mates(outer_slots)
    loglik = after(loglik, outer_slots)
    shares = (loglik, to_mate(loglik, half))
    inner_rows = ((0, HALO, n_rows - 2 * HALO),)
    outer_rows = ((0, 0, HALO), (HALO, n_rows - HALO, HALO))
    (members,) = place(at, after(inner_done, outer_slots), inner_rows, fields.shape)
    members, log_weights = place(at, outer_done, outer_rows, fields.shape, members, shares)
    return log_weights, members


def shards(fields, depth, obs_index, obs_value, obs_var, parent_lookup):
    rows_at = lax.axis_index("rows")
    dom_at = lax.axis_index("dom")
    half = lax.axis_size("dom") // 2
    at = jnp.stack(
        [dom_at % half, rows_at > 0, rows_at < lax.axis_size("rows") - 1, rows_at, dom_at // half, dom_at]
    ).astype(jnp.int32)
    routes, head, tail = prepare(at, parent_lookup, fields, depth, half)
    if half == ROUTED_HALF:
        branches = [(lambda *rest, c=c: cycle(c, *rest)) for c in range(1, half + 1)]
        crossing = jnp.clip(routes[0] - 1, 0, half - 1)
        return lax.switch(crossing, branches, routes, head, tail, at, fields, depth, obs_index, obs_value, obs_var)
    return by_pieces(head, tail, at, fields, depth, obs_index, obs_value, obs_var, parent_lookup)


def by_pieces(head, tail, at, fields, depth, obs_index, obs_value, obs_var, parent_lookup):
    pieces = lax.axis_size("dom")
    n_rows, n_cols = depth.shape
    whole = at * jnp.array([0, 1, 1, 1, 1, 1], jnp.int32)
    (inner,), inner_h = inner_forecast(whole, fields, depth, 1)
    (outer,), outer_h = outer_forecast(whole, fields, depth, *halo_rows(head, tail), 1)
    loglik = misfit(at, obs_index, obs_value, obs_var, inner_h, outer_h)
    log_weights = log_weight(at, sum_over(sum_over(loglik, "dom"), "rows"))
    slab = jnp.concatenate([outer[:, :HALO], inner, outer[:, HALO:]], axis=1)
    tiles = slab.reshape(3, n_rows, pieces, n_cols // pieces).transpose(2, 0, 1, 3)
    received = lax.all_to_all(tiles, "dom", split_axis=0, concat_axis=0, tiled=True)
    picked = jnp.take(received, parent_lookup, axis=0, mode="clip")
    final = lax.all_to_all(picked, "dom", split_axis=0, concat_axis=0, tiled=True)
    return log_weights, final.transpose(1, 2, 0, 3).reshape(1, 3, n_rows, n_cols)


def solution(mesh):
    in_specs = (P("dom", None, "rows", None), P("rows", None), P(), P(), P(), P())
    out_specs = (P("dom"), P("dom", None, "rows", None))
    return jax.shard_map(shards, mesh=mesh, in_specs=in_specs, out_specs=out_specs, check_vma=False)
```

profile of v0, /device:TPU:0, one launch (start us, length us, event | category | flops | bytes accessed | tf_op | source)
XLA Modules:
  0.0 80.4 jit_solution(11005562878487730946)
XLA Ops:
  1.4 2.5 %prepare.1 = (s32[9]{0:T(128)S(1)}, f32[4,8,4096]{2,1,0:T(8,128)S(1)}, f32[4,8,4096]{2,1,0:T(8,128)S(1)}) custom-call(s32[6]{0:T(128)S(1)} %stack.35.refs_0_, s32[8]{0:T(128)S(1)} %copy-done, f32[1,3,32,4096]{3,2,1,0:T(8,128)} %refs_2_.1, f32[32,4096]{1,0:T(8,128)} %refs_3_.1), custom_call_target="tpu_custom_call" | custom-call | tf_op jit(solution)/shard_map/prepare/pallas_call | solution.py:291
  4.0 76.2 %conditional.1 = (f32[1]{0:T(128)}, f32[1,3,32,4096]{3,2,1,0:T(8,128)}) conditional(s32[]{:T(128)} %bitcast.6, (f32[4,8,4096]{2,1,0:T(8,128)S(1)}, f32[4,8,4096]{2,1,0:T(8,128)S(1)}, s32[6]{0:T(128)S(1)}, f32[1,3,32,4096]{3,2,1,0:T(8,128)S(1)}, f32[32,4096]{1,0:T(8,128)S(1)}, /*index=5*/s32[9]{0:T(128)S(1)}, ...), branch_computations={%region_0.1_spmd, %region_1.2_spmd, %region_2.3_spmd, %region_3.4_... | conditional | flops 512 | bytes 19940184 | solution.py:417
  4.0 2.4 %collective-permute-start.21 = (f32[4,8,4096]{2,1,0:T(8,128)S(1)}, f32[4,8,4096]{2,1,0:T(8,128)S(1)}, u32[]{:S(2)}, u32[]{:S(2)}) collective-permute-start(f32[4,8,4096]{2,1,0:T(8,128)S(1)} %get-tuple-element.121), channel_id=1, source_target_pairs={{0,1},{1,2},{2,3},{4,5},{5,6},{6,7},{8,9},{9,10},{10,11},{12,13},{... | collective-permute-start | bytes 1572872 | tf_op jit(solution)/shard_map/cond/branch_1_fun/ppermute | solution.py:355
  7.7 3.9 %inner.5 = (f32[3,16,1024]{2,1,0:T(8,128)S(1)}, f32[3,16,1024]{2,1,0:T(8,128)S(1)}, f32[3,16,1024]{2,1,0:T(8,128)S(1)}, f32[3,16,1024]{2,1,0:T(8,128)S(1)}, f32[16,4096]{1,0:T(8,128)S(1)}) custom-call(s32[6]{0:T(128)S(1)} %get-tuple-element.117.at_ref, f32[1,3,32,4096]{3,2,1,0:T(8,128)S(1)} %get-tuple-element.119.fields_ref, ...), custom_call_target="tpu_custom_call" | custom-call | tf_op jit(solution)/shard_map/cond/branch_1_fun/inner/pallas_call | solution.py:88
  11.6 2.4 %collective-permute-start.26 = (f32[3,16,1024]{2,1,0:T(8,128)S(1)}, f32[3,16,1024]{2,1,0:T(8,128)S(1)}, u32[]{:S(2)}, u32[]{:S(2)}) collective-permute-start(f32[3,16,1024]{2,1,0:T(8,128)S(1)} %get-tuple-element.133), channel_id=1, source_target_pairs={{0,4},{4,0},{8,12},{12,8},{16,20},{20,16},{24,28},{28,24},{1,5},{5... | collective-permute-start | bytes 589832 | tf_op jit(solution)/shard_map/cond/branch_1_fun/ppermute | solution.py:303
  14.0 1.6 %collective-permute-start.27 = (f32[3,16,1024]{2,1,0:T(8,128)S(1)}, f32[3,16,1024]{2,1,0:T(8,128)S(1)}, u32[]{:S(2)}, u32[]{:S(2)}) collective-permute-start(f32[3,16,1024]{2,1,0:T(8,128)S(1)} %get-tuple-element.134), channel_id=1, source_target_pairs={{0,8},{4,12},{8,0},{12,4},{16,24},{20,28},{24,16},{28,20},{1,9},{5... | collective-permute-start | bytes 589832 | tf_op jit(solution)/shard_map/cond/branch_1_fun/ppermute | solution.py:303
  15.6 5.6 %outer.5 = (f32[3,16,1024]{2,1,0:T(8,128)S(1)}, f32[3,16,1024]{2,1,0:T(8,128)S(1)}, f32[3,16,1024]{2,1,0:T(8,128)S(1)}, f32[3,16,1024]{2,1,0:T(8,128)S(1)}, f32[16,4096]{1,0:T(8,128)S(1)}) custom-call(s32[6]{0:T(128)S(1)} %get-tuple-element.117.at_ref, f32[1,3,32,4096]{3,2,1,0:T(8,128)S(1)} %get-tuple-element.119.fields_ref, ...), custom_call_target="tpu_custom_call" | custom-call | tf_op jit(solution)/shard_map/cond/branch_1_fun/outer/pallas_call | solution.py:88
  21.2 2.0 %collective-permute-start.23 = (f32[3,16,1024]{2,1,0:T(8,128)S(1)}, f32[3,16,1024]{2,1,0:T(8,128)S(1)}, u32[]{:S(2)}, u32[]{:S(2)}) collective-permute-start(f32[3,16,1024]{2,1,0:T(8,128)S(1)} %get-tuple-element.124), channel_id=1, source_target_pairs={{0,4},{4,0},{8,12},{12,8},{16,20},{20,16},{24,28},{28,24},{1,5},{5... | collective-permute-start | bytes 589832 | tf_op jit(solution)/shard_map/cond/branch_1_fun/ppermute | solution.py:303
  23.2 1.6 %collective-permute-start.24 = (f32[3,16,1024]{2,1,0:T(8,128)S(1)}, f32[3,16,1024]{2,1,0:T(8,128)S(1)}, u32[]{:S(2)}, u32[]{:S(2)}) collective-permute-start(f32[3,16,1024]{2,1,0:T(8,128)S(1)} %get-tuple-element.125), channel_id=1, source_target_pairs={{0,8},{4,12},{8,0},{12,4},{16,24},{20,28},{24,16},{28,20},{1,9},{5... | collective-permute-start | bytes 589832 | tf_op jit(solution)/shard_map/cond/branch_1_fun/ppermute | solution.py:303
  25.4 3.0 %collective-permute-start.37 = (f32[2,3,16,1024]{3,2,1,0:T(8,128)S(1)}, f32[2,3,16,1024]{3,2,1,0:T(8,128)S(1)}, u32[]{:S(2)}, u32[]{:S(2)}) collective-permute-start(f32[2,3,16,1024]{3,2,1,0:T(8,128)S(1)} %pick.20), channel_id=1, source_target_pairs={{0,16},{4,20},{8,24},{12,28},{16,0},{20,4},{24,8},{28,12},{1,17},{... | collective-permute-start | bytes 1179656 | tf_op jit(solution)/shard_map/cond/branch_1_fun/ppermute | solution.py:303
  28.4 4.4 %misfit.5 = f32[1,128]{1,0:T(1,128)S(1)} custom-call(s32[6]{0:T(128)S(1)} %get-tuple-element.117.at_ref, s32[256]{0:T(256)S(1)} %get-tuple-element.127.index_ref, f32[256]{0:T(256)S(1)} %get-tuple-element.128.value_ref, f32[256]{0:T(256)S(1)} %get-tuple-element.129.var_ref, f32[16,4096]{1,0:T(8,128)S(1)} %get-tuple-element.130.inner_ref, ...), custom_call_target="tpu_custom_call" | custom-call | tf_op jit(solution)/shard_map/cond/branch_1_fun/misfit/pallas_call | solution.py:144
  32.8 2.7 %collective-permute-start.29 = (f32[1,128]{1,0:T(1,128)S(1)}, f32[1,128]{1,0:T(1,128)S(1)}, u32[]{:S(2)}, u32[]{:S(2)}) collective-permute-start(f32[1,128]{1,0:T(1,128)S(1)} %misfit.5), channel_id=1, source_target_pairs={{0,1},{1,0},{2,3},{3,2},{4,5},{5,4},{6,7},{7,6},{8,9},{9,8},{10,11... | collective-permute-start | bytes 1544 | tf_op jit(solution)/shard_map/cond/branch_1_fun/ppermute | solution.py:159
  36.3 1.7 %collective-permute-start.30 = (f32[1,128]{1,0:T(1,128)S(1)}, f32[1,128]{1,0:T(1,128)S(1)}, u32[]{:S(2)}, u32[]{:S(2)}) collective-permute-start(f32[1,128]{1,0:T(1,128)S(1)} %add.42), channel_id=1, source_target_pairs={{0,2},{1,3},{2,0},{3,1},{4,6},{5,7},{6,4},{7,5},{8,10},{9,11},{10,... | collective-permute-start | bytes 1544 | tf_op jit(solution)/shard_map/cond/branch_1_fun/ppermute | solution.py:159
  38.0 1.8 %collective-permute-done.30 = f32[1,128]{1,0:T(1,128)S(1)} collective-permute-done((f32[1,128]{1,0:T(1,128)S(1)}, f32[1,128]{1,0:T(1,128)S(1)}, u32[]{:S(2)}, u32[]{:S(2)}) %collective-permute-start.30) | collective-permute-done | bytes 544 | tf_op jit(solution)/shard_map/cond/branch_1_fun/ppermute | solution.py:159
  41.3 2.1 %collective-permute-done.31 = f32[1,128]{1,0:T(1,128)S(1)} collective-permute-done((f32[1,128]{1,0:T(1,128)S(1)}, f32[1,128]{1,0:T(1,128)S(1)}, u32[]{:S(2)}, u32[]{:S(2)}) %collective-permute-start.31) | collective-permute-done | bytes 544 | tf_op jit(solution)/shard_map/cond/branch_1_fun/ppermute | solution.py:303
  43.4 1.6 %collective-permute-start.32 = (f32[1,128]{1,0:T(1,128)S(1)}, f32[1,128]{1,0:T(1,128)S(1)}, u32[]{:S(2)}, u32[]{:S(2)}) collective-permute-start(f32[1,128]{1,0:T(1,128)S(1)} %add.44), channel_id=1, source_target_pairs={{0,8},{4,12},{8,0},{12,4},{16,24},{20,28},{24,16},{28,20},{1,9},{5... | collective-permute-start | bytes 1544 | tf_op jit(solution)/shard_map/cond/branch_1_fun/ppermute | solution.py:303
  45.0 2.0 %collective-permute-done.32 = f32[1,128]{1,0:T(1,128)S(1)} collective-permute-done((f32[1,128]{1,0:T(1,128)S(1)}, f32[1,128]{1,0:T(1,128)S(1)}, u32[]{:S(2)}, u32[]{:S(2)}) %collective-permute-start.32) | collective-permute-done | bytes 544 | tf_op jit(solution)/shard_map/cond/branch_1_fun/ppermute | solution.py:303
  50.2 1.6 %collective-permute-start.39 = (f32[3,16,1024]{2,1,0:T(8,128)S(1)}, f32[3,16,1024]{2,1,0:T(8,128)S(1)}, u32[]{:S(2)}, u32[]{:S(2)}) collective-permute-start(f32[3,16,1024]{2,1,0:T(8,128)S(1)} %get-tuple-element.152), channel_id=1, source_target_pairs={{0,8},{4,12},{8,0},{12,4},{16,24},{20,28},{24,16},{28,20},{1,9},{5... | collective-permute-start | bytes 589832 | tf_op jit(solution)/shard_map/cond/branch_1_fun/ppermute | solution.py:303
  52.3 13.1 %collective-permute-done.33.refs_4_ = f32[2,3,16,1024]{3,2,1,0:T(8,128)S(1)} collective-permute-done((f32[2,3,16,1024]{3,2,1,0:T(8,128)S(1)}, f32[2,3,16,1024]{3,2,1,0:T(8,128)S(1)}, u32[]{:S(2)}, u32[]{:S(2)}) %collective-permute-start.33) | collective-permute-done | bytes 393248 | tf_op jit(solution)/shard_map/cond/branch_1_fun/ppermute | solution.py:303
  66.1 2.1 %collective-permute-start.34 = (f32[3,16,1024]{2,1,0:T(8,128)S(1)}, f32[3,16,1024]{2,1,0:T(8,128)S(1)}, u32[]{:S(2)}, u32[]{:S(2)}) collective-permute-start(f32[3,16,1024]{2,1,0:T(8,128)S(1)} %get-tuple-element.146), channel_id=1, source_target_pairs={{0,4},{4,0},{8,12},{12,8},{16,20},{20,16},{24,28},{28,24},{1,5},{5... | collective-permute-start | bytes 589832 | tf_op jit(solution)/shard_map/cond/branch_1_fun/ppermute | solution.py:303
  68.2 1.5 %collective-permute-start.36 = (f32[3,16,1024]{2,1,0:T(8,128)S(1)}, f32[3,16,1024]{2,1,0:T(8,128)S(1)}, u32[]{:S(2)}, u32[]{:S(2)}) collective-permute-start(f32[3,16,1024]{2,1,0:T(8,128)S(1)} %get-tuple-element.148), channel_id=1, source_target_pairs={{0,12},{4,8},{8,4},{12,0},{16,28},{20,24},{24,20},{28,16},{1,13},{... | collective-permute-start | bytes 589832 | tf_op jit(solution)/shard_map/cond/branch_1_fun/ppermute | solution.py:303
  72.1 3.9 %collective-permute-done.41.refs_6_ = f32[1,128]{1,0:T(1,128)S(1)} collective-permute-done((f32[1,128]{1,0:T(1,128)S(1)}, f32[1,128]{1,0:T(1,128)S(1)}, u32[]{:S(2)}, u32[]{:S(2)}) %collective-permute-start.41) | collective-permute-done | bytes 544 | tf_op jit(solution)/shard_map/cond/branch_1_fun/ppermute | solution.py:303
  76.0 1.9 %collective-permute-done.36.refs_3_ = f32[3,16,1024]{2,1,0:T(8,128)S(1)} collective-permute-done((f32[3,16,1024]{2,1,0:T(8,128)S(1)}, f32[3,16,1024]{2,1,0:T(8,128)S(1)}, u32[]{:S(2)}, u32[]{:S(2)}) %collective-permute-start.36) | collective-permute-done | bytes 196640 | tf_op jit(solution)/shard_map/cond/branch_1_fun/ppermute | solution.py:303
  77.9 2.0 %place.11 = (f32[1,3,32,4096]{3,2,1,0:T(8,128)}, f32[1]{0:T(128)}) custom-call(s32[6]{0:T(128)S(1)} %get-tuple-element.117.at_ref, f32[3,16,1024]{2,1,0:T(8,128)S(1)} %get-tuple-element.145.refs_0_, f32[3,16,1024]{2,1,0:T(8,128)S(1)} %collective-permute-done.34.refs_1_, ...), custom_call_target="tpu_custom_call", output_to_operand_aliasing={{0}: (5, {})} | custom-call | tf_op jit(solution)/shard_map/cond/branch_1_fun/place/pallas_call | solution.py:218
  (46 shorter events, 11.7 us)
Async XLA Ops:
  0.6 3.3 %copy-start.5 = (f32[256]{0:T(256)S(1)}, f32[256]{0:T(256)}, u32[]{:S(2)}) copy-start(f32[256]{0:T(256)} %param.14) | copy-start | bytes 3076
  0.6 3.3 %copy-start.4 = (f32[256]{0:T(256)S(1)}, f32[256]{0:T(256)}, u32[]{:S(2)}) copy-start(f32[256]{0:T(256)} %param.13) | copy-start | bytes 3076
  0.7 3.3 %copy-start.3 = (s32[256]{0:T(256)S(1)}, s32[256]{0:T(256)}, u32[]{:S(2)}) copy-start(s32[256]{0:T(256)} %param.12) | copy-start | bytes 3076
  4.0 11.6 %collective-permute-start.21 = (f32[4,8,4096]{2,1,0:T(8,128)S(1)}, f32[4,8,4096]{2,1,0:T(8,128)S(1)}, u32[]{:S(2)}, u32[]{:S(2)}) collective-permute-start(f32[4,8,4096]{2,1,0:T(8,128)S(1)} %get-tuple-element.121), channel_id=1, source_target_pairs={{0,1},{1,2},{2,3},{4,5},{5,6},{6,7},{8,9},{9,10},{10,11},{12,13},{... | collective-permute-start | bytes 1572872 | tf_op jit(solution)/shard_map/cond/branch_1_fun/ppermute | solution.py:355
  6.4 9.2 %collective-permute-start.22 = (f32[4,8,4096]{2,1,0:T(8,128)S(1)}, f32[4,8,4096]{2,1,0:T(8,128)S(1)}, u32[]{:S(2)}, u32[]{:S(2)}) collective-permute-start(f32[4,8,4096]{2,1,0:T(8,128)S(1)} %get-tuple-element.122), channel_id=1, source_target_pairs={{1,0},{2,1},{3,2},{5,4},{6,5},{7,6},{9,8},{10,9},{11,10},{13,12},{... | collective-permute-start | bytes 1572872 | tf_op jit(solution)/shard_map/cond/branch_1_fun/ppermute | solution.py:356
  11.6 13.2 %collective-permute-start.26 = (f32[3,16,1024]{2,1,0:T(8,128)S(1)}, f32[3,16,1024]{2,1,0:T(8,128)S(1)}, u32[]{:S(2)}, u32[]{:S(2)}) collective-permute-start(f32[3,16,1024]{2,1,0:T(8,128)S(1)} %get-tuple-element.133), channel_id=1, source_target_pairs={{0,4},{4,0},{8,12},{12,8},{16,20},{20,16},{24,28},{28,24},{1,5},{5... | collective-permute-start | bytes 589832 | tf_op jit(solution)/shard_map/cond/branch_1_fun/ppermute | solution.py:303
  14.0 10.8 %collective-permute-start.27 = (f32[3,16,1024]{2,1,0:T(8,128)S(1)}, f32[3,16,1024]{2,1,0:T(8,128)S(1)}, u32[]{:S(2)}, u32[]{:S(2)}) collective-permute-start(f32[3,16,1024]{2,1,0:T(8,128)S(1)} %get-tuple-element.134), channel_id=1, source_target_pairs={{0,8},{4,12},{8,0},{12,4},{16,24},{20,28},{24,16},{28,20},{1,9},{5... | collective-permute-start | bytes 589832 | tf_op jit(solution)/shard_map/cond/branch_1_fun/ppermute | solution.py:303
  15.6 9.2 %collective-permute-start.28 = (f32[3,16,1024]{2,1,0:T(8,128)S(1)}, f32[3,16,1024]{2,1,0:T(8,128)S(1)}, u32[]{:S(2)}, u32[]{:S(2)}) collective-permute-start(f32[3,16,1024]{2,1,0:T(8,128)S(1)} %get-tuple-element.135), channel_id=1, source_target_pairs={{0,12},{4,8},{8,4},{12,0},{16,28},{20,24},{24,20},{28,16},{1,13},{... | collective-permute-start | bytes 589832 | tf_op jit(solution)/shard_map/cond/branch_1_fun/ppermute | solution.py:303
  21.2 25.8 %collective-permute-start.23 = (f32[3,16,1024]{2,1,0:T(8,128)S(1)}, f32[3,16,1024]{2,1,0:T(8,128)S(1)}, u32[]{:S(2)}, u32[]{:S(2)}) collective-permute-start(f32[3,16,1024]{2,1,0:T(8,128)S(1)} %get-tuple-element.124), channel_id=1, source_target_pairs={{0,4},{4,0},{8,12},{12,8},{16,20},{20,16},{24,28},{28,24},{1,5},{5... | collective-permute-start | bytes 589832 | tf_op jit(solution)/shard_map/cond/branch_1_fun/ppermute | solution.py:303
  23.2 23.8 %collective-permute-start.24 = (f32[3,16,1024]{2,1,0:T(8,128)S(1)}, f32[3,16,1024]{2,1,0:T(8,128)S(1)}, u32[]{:S(2)}, u32[]{:S(2)}) collective-permute-start(f32[3,16,1024]{2,1,0:T(8,128)S(1)} %get-tuple-element.125), channel_id=1, source_target_pairs={{0,8},{4,12},{8,0},{12,4},{16,24},{20,28},{24,16},{28,20},{1,9},{5... | collective-permute-start | bytes 589832 | tf_op jit(solution)/shard_map/cond/branch_1_fun/ppermute | solution.py:303
  24.8 22.2 %collective-permute-start.25 = (f32[3,16,1024]{2,1,0:T(8,128)S(1)}, f32[3,16,1024]{2,1,0:T(8,128)S(1)}, u32[]{:S(2)}, u32[]{:S(2)}) collective-permute-start(f32[3,16,1024]{2,1,0:T(8,128)S(1)} %get-tuple-element.126), channel_id=1, source_target_pairs={{0,12},{4,8},{8,4},{12,0},{16,28},{20,24},{24,20},{28,16},{1,13},{... | collective-permute-start | bytes 589832 | tf_op jit(solution)/shard_map/cond/branch_1_fun/ppermute | solution.py:303
  25.4 22.6 %collective-permute-start.37 = (f32[2,3,16,1024]{3,2,1,0:T(8,128)S(1)}, f32[2,3,16,1024]{3,2,1,0:T(8,128)S(1)}, u32[]{:S(2)}, u32[]{:S(2)}) collective-permute-start(f32[2,3,16,1024]{3,2,1,0:T(8,128)S(1)} %pick.20), channel_id=1, source_target_pairs={{0,16},{4,20},{8,24},{12,28},{16,0},{20,4},{24,8},{28,12},{1,17},{... | collective-permute-start | bytes 1179656 | tf_op jit(solution)/shard_map/cond/branch_1_fun/ppermute | solution.py:303
  32.8 3.5 %collective-permute-start.29 = (f32[1,128]{1,0:T(1,128)S(1)}, f32[1,128]{1,0:T(1,128)S(1)}, u32[]{:S(2)}, u32[]{:S(2)}) collective-permute-start(f32[1,128]{1,0:T(1,128)S(1)} %misfit.5), channel_id=1, source_target_pairs={{0,1},{1,0},{2,3},{3,2},{4,5},{5,4},{6,7},{7,6},{8,9},{9,8},{10,11... | collective-permute-start | bytes 1544 | tf_op jit(solution)/shard_map/cond/branch_1_fun/ppermute | solution.py:159
  36.3 3.5 %collective-permute-start.30 = (f32[1,128]{1,0:T(1,128)S(1)}, f32[1,128]{1,0:T(1,128)S(1)}, u32[]{:S(2)}, u32[]{:S(2)}) collective-permute-start(f32[1,128]{1,0:T(1,128)S(1)} %add.42), channel_id=1, source_target_pairs={{0,2},{1,3},{2,0},{3,1},{4,6},{5,7},{6,4},{7,5},{8,10},{9,11},{10,... | collective-permute-start | bytes 1544 | tf_op jit(solution)/shard_map/cond/branch_1_fun/ppermute | solution.py:159
  39.9 3.5 %collective-permute-start.31 = (f32[1,128]{1,0:T(1,128)S(1)}, f32[1,128]{1,0:T(1,128)S(1)}, u32[]{:S(2)}, u32[]{:S(2)}) collective-permute-start(f32[1,128]{1,0:T(1,128)S(1)} %add.43), channel_id=1, source_target_pairs={{0,4},{4,0},{8,12},{12,8},{16,20},{20,16},{24,28},{28,24},{1,5},{5... | collective-permute-start | bytes 1544 | tf_op jit(solution)/shard_map/cond/branch_1_fun/ppermute | solution.py:303
  43.4 3.5 %collective-permute-start.32 = (f32[1,128]{1,0:T(1,128)S(1)}, f32[1,128]{1,0:T(1,128)S(1)}, u32[]{:S(2)}, u32[]{:S(2)}) collective-permute-start(f32[1,128]{1,0:T(1,128)S(1)} %add.44), channel_id=1, source_target_pairs={{0,8},{4,12},{8,0},{12,4},{16,24},{20,28},{24,16},{28,20},{1,9},{5... | collective-permute-start | bytes 1544 | tf_op jit(solution)/shard_map/cond/branch_1_fun/ppermute | solution.py:303
  47.6 17.8 %collective-permute-start.33 = (f32[2,3,16,1024]{3,2,1,0:T(8,128)S(1)}, f32[2,3,16,1024]{3,2,1,0:T(8,128)S(1)}, u32[]{:S(2)}, u32[]{:S(2)}) collective-permute-start(f32[2,3,16,1024]{3,2,1,0:T(8,128)S(1)} %pick.21), channel_id=1, source_target_pairs={{0,16},{4,20},{8,24},{12,28},{16,0},{20,4},{24,8},{28,12},{1,17},{... | collective-permute-start | bytes 1179656 | tf_op jit(solution)/shard_map/cond/branch_1_fun/ppermute | solution.py:303
  48.7 19.4 %collective-permute-start.38 = (f32[3,16,1024]{2,1,0:T(8,128)S(1)}, f32[3,16,1024]{2,1,0:T(8,128)S(1)}, u32[]{:S(2)}, u32[]{:S(2)}) collective-permute-start(f32[3,16,1024]{2,1,0:T(8,128)S(1)} %get-tuple-element.151), channel_id=1, source_target_pairs={{0,4},{4,0},{8,12},{12,8},{16,20},{20,16},{24,28},{28,24},{1,5},{5... | collective-permute-start | bytes 589832 | tf_op jit(solution)/shard_map/cond/branch_1_fun/ppermute | solution.py:303
  50.2 19.5 %collective-permute-start.39 = (f32[3,16,1024]{2,1,0:T(8,128)S(1)}, f32[3,16,1024]{2,1,0:T(8,128)S(1)}, u32[]{:S(2)}, u32[]{:S(2)}) collective-permute-start(f32[3,16,1024]{2,1,0:T(8,128)S(1)} %get-tuple-element.152), channel_id=1, source_target_pairs={{0,8},{4,12},{8,0},{12,4},{16,24},{20,28},{24,16},{28,20},{1,9},{5... | collective-permute-start | bytes 589832 | tf_op jit(solution)/shard_map/cond/branch_1_fun/ppermute | solution.py:303
  51.8 18.8 %collective-permute-start.40 = (f32[3,16,1024]{2,1,0:T(8,128)S(1)}, f32[3,16,1024]{2,1,0:T(8,128)S(1)}, u32[]{:S(2)}, u32[]{:S(2)}) collective-permute-start(f32[3,16,1024]{2,1,0:T(8,128)S(1)} %get-tuple-element.153), channel_id=1, source_target_pairs={{0,12},{4,8},{8,4},{12,0},{16,28},{20,24},{24,20},{28,16},{1,13},{... | collective-permute-start | bytes 589832 | tf_op jit(solution)/shard_map/cond/branch_1_fun/ppermute | solution.py:303
  66.1 9.9 %collective-permute-start.34 = (f32[3,16,1024]{2,1,0:T(8,128)S(1)}, f32[3,16,1024]{2,1,0:T(8,128)S(1)}, u32[]{:S(2)}, u32[]{:S(2)}) collective-permute-start(f32[3,16,1024]{2,1,0:T(8,128)S(1)} %get-tuple-element.146), channel_id=1, source_target_pairs={{0,4},{4,0},{8,12},{12,8},{16,20},{20,16},{24,28},{28,24},{1,5},{5... | collective-permute-start | bytes 589832 | tf_op jit(solution)/shard_map/cond/branch_1_fun/ppermute | solution.py:303
  68.2 7.9 %collective-permute-start.35 = (f32[3,16,1024]{2,1,0:T(8,128)S(1)}, f32[3,16,1024]{2,1,0:T(8,128)S(1)}, u32[]{:S(2)}, u32[]{:S(2)}) collective-permute-start(f32[3,16,1024]{2,1,0:T(8,128)S(1)} %get-tuple-element.147), channel_id=1, source_target_pairs={{0,8},{4,12},{8,0},{12,4},{16,24},{20,28},{24,16},{28,20},{1,9},{5... | collective-permute-start | bytes 589832 | tf_op jit(solution)/shard_map/cond/branch_1_fun/ppermute | solution.py:303
  68.2 9.8 %collective-permute-start.36 = (f32[3,16,1024]{2,1,0:T(8,128)S(1)}, f32[3,16,1024]{2,1,0:T(8,128)S(1)}, u32[]{:S(2)}, u32[]{:S(2)}) collective-permute-start(f32[3,16,1024]{2,1,0:T(8,128)S(1)} %get-tuple-element.148), channel_id=1, source_target_pairs={{0,12},{4,8},{8,4},{12,0},{16,28},{20,24},{24,20},{28,16},{1,13},{... | collective-permute-start | bytes 589832 | tf_op jit(solution)/shard_map/cond/branch_1_fun/ppermute | solution.py:303
  69.7 6.3 %collective-permute-start.41 = (f32[1,128]{1,0:T(1,128)S(1)}, f32[1,128]{1,0:T(1,128)S(1)}, u32[]{:S(2)}, u32[]{:S(2)}) collective-permute-start(f32[1,128]{1,0:T(1,128)S(1)} %add.45.refs_5_), channel_id=1, source_target_pairs={{0,16},{4,20},{8,24},{12,28},{16,0},{20,4},{24,8},{28,12},{1,17},{... | collective-permute-start | bytes 1544 | tf_op jit(solution)/shard_map/cond/branch_1_fun/ppermute | solution.py:303
  (3 other events, 5.7 us)
where the time goes:
time: 80.8 us; the launch traced here: 80.4 us
  starting transfers between devices  30.1 us (37%)
  waiting for transfers between devices  25.7 us (32%)
  Pallas kernels  22.4 us (28%)
  between operations  0.97 us (1%)
    ppermute x17, waiting for transfers between devices, to_mate(): lax.ppermute(x, 'dom', [(i, i ^ m) for i in range(lax.axis_size('dom'))])  23 us
    ppermute x17, starting transfers between devices, to_mate(): lax.ppermute(x, 'dom', [(i, i ^ m) for i in range(lax.axis_size('dom'))])  22.1 us
    pallas_call x2, Pallas kernels, forecast(): pl.pallas_call(kernel, out_shape=[jax.ShapeDtypeStruct(shape, jnp.float32...  9.49 us
    pallas_call x1, Pallas kernels, misfit(): pl.pallas_call(misfit_kernel, out_shape=jax.ShapeDtypeStruct((1, LANES),...  4.41 us
    ppermute x2, starting transfers between devices, sum_over(): x = x + lax.ppermute(x, axis, [(i, i ^ step) for i in range(count)])  4.35 us
    pallas_call x2, Pallas kernels, place(): pl.pallas_call(kernel, out_shape=out_shape, in_specs=[in_smem] + [in_vmem...  3.44 us
    ppermute x2, waiting for transfers between devices, sum_over(): x = x + lax.ppermute(x, axis, [(i, i ^ step) for i in range(count)])  2.66 us
    pallas_call x4, Pallas kernels, pick(): pl.pallas_call(kernel, out_shape=[jax.ShapeDtypeStruct(shape, jnp.float32...  2.61 us
  transfers between devices with their start and end apart: 21, of which 7 were waited for; matrix products, arithmetic and copies ran while one was open for 0% of the time, Pallas kernels for 22%

commit v1 on v0

--- a/solution.py
+++ b/solution.py
@@ -21,8 +21,6 @@
 
 def model_steps(h_ref, u_ref, v_ref, d_ref, top_open=None, bottom_open=None):
     n_rows, n_cols = h_ref.shape
-    h_ref[...] = h_ref[...] * (0.5 * time_step)
-    d_ref[...] = d_ref[...] * (0.25 * time_step * time_step)
 
     def cols(a):
         return pltpu.roll(a, n_cols - 1, 1) - pltpu.roll(a, 1, 1)
@@ -46,7 +44,14 @@
         return carry
 
     lax.fori_loop(0, STEPS, step, 0)
-    h_ref[...] = h_ref[...] * (2.0 / time_step)
+
+
+def held(k, field):
+    return field * {0: 0.5 * time_step, 3: 0.25 * time_step * time_step}[k] if k in (0, 3) else field
+
+
+def freed(k, field):
+    return field * (2.0 / time_step) if k == 0 else field
 
 
 def store_pieces(at_ref, outs, state, rows_of):
@@ -54,16 +59,16 @@
     for m, out in enumerate(outs):
         start = pl.multiple_of(jnp.bitwise_xor(at_ref[0], m) * width, LANES)
         for k, ref in enumerate(state[:3]):
-            out[k] = rows_of(ref, pl.ds(start, width))
+            out[k] = freed(k, rows_of(ref, pl.ds(start, width)))
 
 
 def inner_kernel(at_ref, fields_ref, depth_ref, *refs):
     outs, h_ref, state = refs[:-5], refs[-5], refs[-4:]
     n_rows = depth_ref.shape[0]
     for k in range(4):
-        state[k][...] = depth_ref[...] if k == 3 else fields_ref[0, k]
+        state[k][...] = held(k, depth_ref[...] if k == 3 else fields_ref[0, k])
     model_steps(*state)
-    h_ref[...] = state[0][HALO : n_rows - HALO]
+    h_ref[...] = freed(0, state[0][HALO : n_rows - HALO])
     store_pieces(at_ref, outs, state, lambda ref, at: ref[HALO : n_rows - HALO, at])
 
 
@@ -71,15 +76,15 @@
     outs, h_ref, state = refs[:-5], refs[-5], refs[-4:]
     n_rows = depth_ref.shape[0]
     for k in range(4):
-        state[k][:HALO] = above_ref[k]
-        state[k][HALO : HALO + n_rows] = depth_ref[...] if k == 3 else fields_ref[0, k]
-        state[k][HALO + n_rows :] = below_ref[k]
+        state[k][:HALO] = held(k, above_ref[k])
+        state[k][HALO : HALO + n_rows] = held(k, depth_ref[...] if k == 3 else fields_ref[0, k])
+        state[k][HALO + n_rows :] = held(k, below_ref[k])
     model_steps(*state, at_ref[1].astype(jnp.float32), at_ref[2].astype(jnp.float32))
 
     def outer_rows(ref, at):
         return jnp.concatenate([ref[HALO : 2 * HALO, at], ref[n_rows : n_rows + HALO, at]], axis=0)
 
-    h_ref[...] = outer_rows(state[0], pl.ds(0, depth_ref.shape[1]))
+    h_ref[...] = freed(0, outer_rows(state[0], pl.ds(0, depth_ref.shape[1])))
     store_pieces(at_ref, outs, state, outer_rows)
 
 
@@ -183,9 +188,10 @@
     )(at, loglik)
 
 
-def place(at, pieces, spans, shape, into=None, shares=()):
+def place(at, pieces, spans, shape, into=None, shares=(), offset=0):
     count = len(pieces)
-    width = shape[-1] // count
+    width = pieces[0].shape[-1]
+    stride = shape[-1] // count
     particles = lax.axis_size("dom")
 
     def kernel(at_ref, *refs):
@@ -194,7 +200,7 @@
         sems = refs[-1]
         copies = []
         for m in range(count):
-            first = pl.multiple_of(jnp.bitwise_xor(at_ref[0], m) * width, LANES)
+            first = pl.multiple_of(jnp.bitwise_xor(at_ref[0], m) * stride + offset, LANES)
             for s, (src_row, dst_row, size) in enumerate(spans):
                 copies.append(
                     pltpu.make_async_copy(
@@ -227,8 +233,10 @@
     )(at, *pieces, *extra, *shares)
 
 
-def prepare_kernel(at_ref, parents_ref, fields_ref, depth_ref, routes_ref, head_ref, tail_ref, sems, *, half):
+def prepare_kernel(at_ref, parents_ref, fields_ref, depth_ref, routes_ref, head_ref, tail_ref, table_ref, sems, *, half):
     n_rows = depth_ref.shape[0]
+    table = pltpu.make_async_copy(parents_ref, table_ref, sems.at[4])
+    table.start()
     copies = []
     for ref, first in ((head_ref, 0), (tail_ref, n_rows - HALO)):
         rows = pl.ds(first, HALO)
@@ -236,8 +244,9 @@
         copies.append(pltpu.make_async_copy(depth_ref.at[rows], ref.at[3], sems.at[len(copies)]))
     for c in copies:
         c.start()
+    table.wait()
     if half <= ROUTED_HALF:
-        route(at_ref, parents_ref, routes_ref, half)
+        route(at_ref, table_ref, routes_ref, half)
     for c in copies:
         c.wait()
 
@@ -291,9 +300,9 @@
     return pl.pallas_call(
         lambda *refs: prepare_kernel(*refs, half=half),
         out_shape=[jax.ShapeDtypeStruct((1 + 2 * half,), jnp.int32), rim, rim],
-        in_specs=[in_smem, in_smem, in_hbm, in_hbm],
+        in_specs=[in_smem, in_hbm, in_hbm, in_hbm],
         out_specs=[in_smem, in_vmem, in_vmem],
-        scratch_shapes=[pltpu.SemaphoreType.DMA((4,))],
+        scratch_shapes=[pltpu.SMEM(parent_lookup.shape, jnp.int32), pltpu.SemaphoreType.DMA((5,))],
         compiler_params=pltpu.CompilerParams(vmem_limit_bytes=VMEM_BYTES),
         name="prepare",
     )(at, parent_lookup, fields, depth)
@@ -307,8 +316,9 @@
     return [x if m == 0 else to_mate(x, m) for m, x in enumerate(pieces)]
 
 
-def pick(routes, first, count, sources, stacks=(), stacked=False, cost=None):
-    block = sources[0].shape
+def pick(routes, first, count, sources, stacks=(), stacked=False, cost=None, columns=None):
+    start, width = columns or (0, sources[0].shape[-1])
+    block = sources[0].shape[:-1] + (width,)
 
     def kernel(routes_ref, *refs):
         n_in = len(sources) + len(stacks)
@@ -320,7 +330,7 @@
 
                 @pl.when(which == s)
                 def _(m=m, src=src, k=k):
-                    value = src[...] if k is None else src[k]
+                    value = src[:, :, start : start + width] if k is None else src[k]
                     if stacked:
                         refs[n_in][m] = value
                     else:
@@ -338,12 +348,12 @@
     )(routes, *sources, *stacks)
 
 
-def chosen(held, routes, crossing, cost=None):
-    return pick(routes, 1, crossing, held, stacked=True, cost=cost)[0]
-
-
-def for_slots(held, got, routes):
-    return pick(routes, 1 + len(held), len(held), held, [got])
+def chosen(pieces, routes, crossing, columns=None):
+    return pick(routes, 1, crossing, pieces, stacked=True, columns=columns)[0]
+
+
+def for_slots(own, got, routes, columns=None):
+    return pick(routes, 1 + len(own), len(own), own, [got], columns=columns)
 
 
 def after(x, *earlier):
@@ -387,19 +397,26 @@
         loglik = loglik + to_mate(loglik, step)
         step *= 2
     outer_ready = after(outer_held, loglik) if rows_first else after(outer_held, loglik, inner_got)
-    outer_chosen = chosen(outer_ready, routes, crossing)
-    outer_got = to_mate(outer_chosen, half)
-    inner_done = among_mates(for_slots(inner_held, after(inner_got, outer_chosen), routes))
+    width = n_cols // half
+    parts = [(0, width // 2), (width // 2, width // 2)] if crossing > 2 else [(0, width)]
+    outer_chosen = [chosen(outer_ready, routes, crossing, columns) for columns in parts]
+    outer_got = [to_mate(x, half) for x in outer_chosen]
+    inner_done = among_mates(for_slots(inner_held, after(inner_got, *outer_chosen), routes))
     if not rows_first:
-        loglik = sum_over(after(loglik, outer_chosen), "rows")
-    outer_slots = for_slots(outer_held, outer_got, routes)
-    outer_done = among_mates(outer_slots)
-    loglik = after(loglik, outer_slots)
+        loglik = sum_over(after(loglik, *outer_chosen), "rows")
+    slots = []
+    outer_done = []
+    for got, columns in zip(outer_got, parts):
+        slots.append(for_slots(outer_held, after(got, *slots), routes, columns))
+        outer_done.append(among_mates(slots[-1]))
+    loglik = after(loglik, slots[-1])
     shares = (loglik, to_mate(loglik, half))
     inner_rows = ((0, HALO, n_rows - 2 * HALO),)
     outer_rows = ((0, 0, HALO), (HALO, n_rows - HALO, HALO))
-    (members,) = place(at, after(inner_done, outer_slots), inner_rows, fields.shape)
-    members, log_weights = place(at, outer_done, outer_rows, fields.shape, members, shares)
+    (members,) = place(at, after(inner_done, slots[-1]), inner_rows, fields.shape)
+    for done, (start, _) in zip(outer_done[:-1], parts):
+        (members,) = place(at, done, outer_rows, fields.shape, members, (), start)
+    members, log_weights = place(at, outer_done[-1], outer_rows, fields.shape, members, shares, parts[-1][0])
     return log_weights, members
 
 

time: 80.8 us -> 80.5 us (level)
  no operation moved by 1% of the time
where the time goes in v1:
time: 80.5 us; the launch traced here: 80.4 us
  starting transfers between devices  29.9 us (37%)
  waiting for transfers between devices  26.1 us (32%)
  Pallas kernels  22.3 us (28%)
  between operations  0.97 us (1%)
    ppermute x17, waiting for transfers between devices, to_mate(): lax.ppermute(x, 'dom', [(i, i ^ m) for i in range(lax.axis_size('dom'))])  23.3 us
    ppermute x17, starting transfers between devices, to_mate(): lax.ppermute(x, 'dom', [(i, i ^ m) for i in range(lax.axis_size('dom'))])  21.8 us
    pallas_call x2, Pallas kernels, forecast(): pl.pallas_call(kernel, out_shape=[jax.ShapeDtypeStruct(shape, jnp.float32...  9.26 us
    pallas_call x1, Pallas kernels, misfit(): pl.pallas_call(misfit_kernel, out_shape=jax.ShapeDtypeStruct((1, LANES),...  4.48 us
    ppermute x2, starting transfers between devices, sum_over(): x = x + lax.ppermute(x, axis, [(i, i ^ step) for i in range(count)])  4.4 us
    pallas_call x2, Pallas kernels, place(): pl.pallas_call(kernel, out_shape=out_shape, in_specs=[in_smem] + [in_vmem...  3.44 us
    ppermute x2, waiting for transfers between devices, sum_over(): x = x + lax.ppermute(x, axis, [(i, i ^ step) for i in range(count)])  2.74 us
    pallas_call x4, Pallas kernels, pick(): pl.pallas_call(kernel, out_shape=[jax.ShapeDtypeStruct(shape, jnp.float32...  2.61 us
  transfers between devices with their start and end apart: 21, of which 7 were waited for; matrix products, arithmetic and copies ran while one was open for 0% of the time, Pallas kernels for 22%

profile of v1, /device:TPU:0, one launch (start us, length us, event | category | flops | bytes accessed | tf_op | source)
XLA Modules:
  0.0 80.4 jit_solution(10155993039566553329)
XLA Ops:
  1.4 2.5 %prepare.1 = (s32[9]{0:T(128)S(1)}, f32[4,8,4096]{2,1,0:T(8,128)S(1)}, f32[4,8,4096]{2,1,0:T(8,128)S(1)}) custom-call(s32[6]{0:T(128)S(1)} %stack.35.refs_0_, s32[8]{0:T(128)S(1)} %copy-done, f32[1,3,32,4096]{3,2,1,0:T(8,128)} %refs_2_.1, f32[32,4096]{1,0:T(8,128)} %refs_3_.1), custom_call_target="tpu_custom_call" | custom-call | tf_op jit(solution)/shard_map/prepare/pallas_call | solution.py:300
  4.0 76.2 %conditional.1 = (f32[1]{0:T(128)}, f32[1,3,32,4096]{3,2,1,0:T(8,128)}) conditional(s32[]{:T(128)} %bitcast.6, (f32[4,8,4096]{2,1,0:T(8,128)S(1)}, f32[4,8,4096]{2,1,0:T(8,128)S(1)}, s32[6]{0:T(128)S(1)}, f32[1,3,32,4096]{3,2,1,0:T(8,128)S(1)}, f32[32,4096]{1,0:T(8,128)S(1)}, /*index=5*/s32[9]{0:T(128)S(1)}, ...), branch_computations={%region_0.1_spmd, %region_1.2_spmd, %region_2.3_spmd, %region_3.4_... | conditional | flops 512 | bytes 19940344 | solution.py:434
  4.0 2.4 %collective-permute-start.21 = (f32[4,8,4096]{2,1,0:T(8,128)S(1)}, f32[4,8,4096]{2,1,0:T(8,128)S(1)}, u32[]{:S(2)}, u32[]{:S(2)}) collective-permute-start(f32[4,8,4096]{2,1,0:T(8,128)S(1)} %get-tuple-element.121), channel_id=1, source_target_pairs={{0,1},{1,2},{2,3},{4,5},{5,6},{6,7},{8,9},{9,10},{10,11},{12,13},{... | collective-permute-start | bytes 1572872 | tf_op jit(solution)/shard_map/cond/branch_1_fun/ppermute | solution.py:365
  7.7 3.8 %inner.5 = (f32[3,16,1024]{2,1,0:T(8,128)S(1)}, f32[3,16,1024]{2,1,0:T(8,128)S(1)}, f32[3,16,1024]{2,1,0:T(8,128)S(1)}, f32[3,16,1024]{2,1,0:T(8,128)S(1)}, f32[16,4096]{1,0:T(8,128)S(1)}) custom-call(s32[6]{0:T(128)S(1)} %get-tuple-element.117.at_ref, f32[1,3,32,4096]{3,2,1,0:T(8,128)S(1)} %get-tuple-element.119.fields_ref, ...), custom_call_target="tpu_custom_call" | custom-call | tf_op jit(solution)/shard_map/cond/branch_1_fun/inner/pallas_call | solution.py:93
  11.5 2.4 %collective-permute-start.26 = (f32[3,16,1024]{2,1,0:T(8,128)S(1)}, f32[3,16,1024]{2,1,0:T(8,128)S(1)}, u32[]{:S(2)}, u32[]{:S(2)}) collective-permute-start(f32[3,16,1024]{2,1,0:T(8,128)S(1)} %get-tuple-element.133), channel_id=1, source_target_pairs={{0,4},{4,0},{8,12},{12,8},{16,20},{20,16},{24,28},{28,24},{1,5},{5... | collective-permute-start | bytes 589832 | tf_op jit(solution)/shard_map/cond/branch_1_fun/ppermute | solution.py:312
  13.9 1.6 %collective-permute-start.27 = (f32[3,16,1024]{2,1,0:T(8,128)S(1)}, f32[3,16,1024]{2,1,0:T(8,128)S(1)}, u32[]{:S(2)}, u32[]{:S(2)}) collective-permute-start(f32[3,16,1024]{2,1,0:T(8,128)S(1)} %get-tuple-element.134), channel_id=1, source_target_pairs={{0,8},{4,12},{8,0},{12,4},{16,24},{20,28},{24,16},{28,20},{1,9},{5... | collective-permute-start | bytes 589832 | tf_op jit(solution)/shard_map/cond/branch_1_fun/ppermute | solution.py:312
  15.5 5.5 %outer.5 = (f32[3,16,1024]{2,1,0:T(8,128)S(1)}, f32[3,16,1024]{2,1,0:T(8,128)S(1)}, f32[3,16,1024]{2,1,0:T(8,128)S(1)}, f32[3,16,1024]{2,1,0:T(8,128)S(1)}, f32[16,4096]{1,0:T(8,128)S(1)}) custom-call(s32[6]{0:T(128)S(1)} %get-tuple-element.117.at_ref, f32[1,3,32,4096]{3,2,1,0:T(8,128)S(1)} %get-tuple-element.119.fields_ref, ...), custom_call_target="tpu_custom_call" | custom-call | tf_op jit(solution)/shard_map/cond/branch_1_fun/outer/pallas_call | solution.py:93
  21.0 2.0 %collective-permute-start.23 = (f32[3,16,1024]{2,1,0:T(8,128)S(1)}, f32[3,16,1024]{2,1,0:T(8,128)S(1)}, u32[]{:S(2)}, u32[]{:S(2)}) collective-permute-start(f32[3,16,1024]{2,1,0:T(8,128)S(1)} %get-tuple-element.124), channel_id=1, source_target_pairs={{0,4},{4,0},{8,12},{12,8},{16,20},{20,16},{24,28},{28,24},{1,5},{5... | collective-permute-start | bytes 589832 | tf_op jit(solution)/shard_map/cond/branch_1_fun/ppermute | solution.py:312
  23.0 1.6 %collective-permute-start.24 = (f32[3,16,1024]{2,1,0:T(8,128)S(1)}, f32[3,16,1024]{2,1,0:T(8,128)S(1)}, u32[]{:S(2)}, u32[]{:S(2)}) collective-permute-start(f32[3,16,1024]{2,1,0:T(8,128)S(1)} %get-tuple-element.125), channel_id=1, source_target_pairs={{0,8},{4,12},{8,0},{12,4},{16,24},{20,28},{24,16},{28,20},{1,9},{5... | collective-permute-start | bytes 589832 | tf_op jit(solution)/shard_map/cond/branch_1_fun/ppermute | solution.py:312
  25.2 3.0 %collective-permute-start.37 = (f32[2,3,16,1024]{3,2,1,0:T(8,128)S(1)}, f32[2,3,16,1024]{3,2,1,0:T(8,128)S(1)}, u32[]{:S(2)}, u32[]{:S(2)}) collective-permute-start(f32[2,3,16,1024]{3,2,1,0:T(8,128)S(1)} %pick.24), channel_id=1, source_target_pairs={{0,16},{4,20},{8,24},{12,28},{16,0},{20,4},{24,8},{28,12},{1,17},{... | collective-permute-start | bytes 1179656 | tf_op jit(solution)/shard_map/cond/branch_1_fun/ppermute | solution.py:312
  28.2 4.5 %misfit.5 = f32[1,128]{1,0:T(1,128)S(1)} custom-call(s32[6]{0:T(128)S(1)} %get-tuple-element.117.at_ref, s32[256]{0:T(256)S(1)} %get-tuple-element.127.index_ref, f32[256]{0:T(256)S(1)} %get-tuple-element.128.value_ref, f32[256]{0:T(256)S(1)} %get-tuple-element.129.var_ref, f32[16,4096]{1,0:T(8,128)S(1)} %get-tuple-element.130.inner_ref, ...), custom_call_target="tpu_custom_call" | custom-call | tf_op jit(solution)/shard_map/cond/branch_1_fun/misfit/pallas_call | solution.py:149
  32.7 2.8 %collective-permute-start.29 = (f32[1,128]{1,0:T(1,128)S(1)}, f32[1,128]{1,0:T(1,128)S(1)}, u32[]{:S(2)}, u32[]{:S(2)}) collective-permute-start(f32[1,128]{1,0:T(1,128)S(1)} %misfit.5), channel_id=1, source_target_pairs={{0,1},{1,0},{2,3},{3,2},{4,5},{5,4},{6,7},{7,6},{8,9},{9,8},{10,11... | collective-permute-start | bytes 1544 | tf_op jit(solution)/shard_map/cond/branch_1_fun/ppermute | solution.py:164
  36.3 1.6 %collective-permute-start.30 = (f32[1,128]{1,0:T(1,128)S(1)}, f32[1,128]{1,0:T(1,128)S(1)}, u32[]{:S(2)}, u32[]{:S(2)}) collective-permute-start(f32[1,128]{1,0:T(1,128)S(1)} %add.42), channel_id=1, source_target_pairs={{0,2},{1,3},{2,0},{3,1},{4,6},{5,7},{6,4},{7,5},{8,10},{9,11},{10,... | collective-permute-start | bytes 1544 | tf_op jit(solution)/shard_map/cond/branch_1_fun/ppermute | solution.py:164
  37.9 1.9 %collective-permute-done.30 = f32[1,128]{1,0:T(1,128)S(1)} collective-permute-done((f32[1,128]{1,0:T(1,128)S(1)}, f32[1,128]{1,0:T(1,128)S(1)}, u32[]{:S(2)}, u32[]{:S(2)}) %collective-permute-start.30) | collective-permute-done | bytes 544 | tf_op jit(solution)/shard_map/cond/branch_1_fun/ppermute | solution.py:164
  41.3 2.1 %collective-permute-done.31 = f32[1,128]{1,0:T(1,128)S(1)} collective-permute-done((f32[1,128]{1,0:T(1,128)S(1)}, f32[1,128]{1,0:T(1,128)S(1)}, u32[]{:S(2)}, u32[]{:S(2)}) %collective-permute-start.31) | collective-permute-done | bytes 544 | tf_op jit(solution)/shard_map/cond/branch_1_fun/ppermute | solution.py:312
  43.4 1.6 %collective-permute-start.32 = (f32[1,128]{1,0:T(1,128)S(1)}, f32[1,128]{1,0:T(1,128)S(1)}, u32[]{:S(2)}, u32[]{:S(2)}) collective-permute-start(f32[1,128]{1,0:T(1,128)S(1)} %add.44), channel_id=1, source_target_pairs={{0,8},{4,12},{8,0},{12,4},{16,24},{20,28},{24,16},{28,20},{1,9},{5... | collective-permute-start | bytes 1544 | tf_op jit(solution)/shard_map/cond/branch_1_fun/ppermute | solution.py:312
  45.0 2.0 %collective-permute-done.32 = f32[1,128]{1,0:T(1,128)S(1)} collective-permute-done((f32[1,128]{1,0:T(1,128)S(1)}, f32[1,128]{1,0:T(1,128)S(1)}, u32[]{:S(2)}, u32[]{:S(2)}) %collective-permute-start.32) | collective-permute-done | bytes 544 | tf_op jit(solution)/shard_map/cond/branch_1_fun/ppermute | solution.py:312
  50.1 1.6 %collective-permute-start.39 = (f32[3,16,1024]{2,1,0:T(8,128)S(1)}, f32[3,16,1024]{2,1,0:T(8,128)S(1)}, u32[]{:S(2)}, u32[]{:S(2)}) collective-permute-start(f32[3,16,1024]{2,1,0:T(8,128)S(1)} %get-tuple-element.152), channel_id=1, source_target_pairs={{0,8},{4,12},{8,0},{12,4},{16,24},{20,28},{24,16},{28,20},{1,9},{5... | collective-permute-start | bytes 589832 | tf_op jit(solution)/shard_map/cond/branch_1_fun/ppermute | solution.py:312
  52.2 13.1 %collective-permute-done.33.refs_4_ = f32[2,3,16,1024]{3,2,1,0:T(8,128)S(1)} collective-permute-done((f32[2,3,16,1024]{3,2,1,0:T(8,128)S(1)}, f32[2,3,16,1024]{3,2,1,0:T(8,128)S(1)}, u32[]{:S(2)}, u32[]{:S(2)}) %collective-permute-start.33) | collective-permute-done | bytes 393248 | tf_op jit(solution)/shard_map/cond/branch_1_fun/ppermute | solution.py:312
  66.1 2.0 %collective-permute-start.34 = (f32[3,16,1024]{2,1,0:T(8,128)S(1)}, f32[3,16,1024]{2,1,0:T(8,128)S(1)}, u32[]{:S(2)}, u32[]{:S(2)}) collective-permute-start(f32[3,16,1024]{2,1,0:T(8,128)S(1)} %get-tuple-element.146), channel_id=1, source_target_pairs={{0,4},{4,0},{8,12},{12,8},{16,20},{20,16},{24,28},{28,24},{1,5},{5... | collective-permute-start | bytes 589832 | tf_op jit(solution)/shard_map/cond/branch_1_fun/ppermute | solution.py:312
  68.1 1.6 %collective-permute-start.36 = (f32[3,16,1024]{2,1,0:T(8,128)S(1)}, f32[3,16,1024]{2,1,0:T(8,128)S(1)}, u32[]{:S(2)}, u32[]{:S(2)}) collective-permute-start(f32[3,16,1024]{2,1,0:T(8,128)S(1)} %get-tuple-element.148), channel_id=1, source_target_pairs={{0,12},{4,8},{8,4},{12,0},{16,28},{20,24},{24,20},{28,16},{1,13},{... | collective-permute-start | bytes 589832 | tf_op jit(solution)/shard_map/cond/branch_1_fun/ppermute | solution.py:312
  71.8 4.1 %collective-permute-done.41.refs_6_ = f32[1,128]{1,0:T(1,128)S(1)} collective-permute-done((f32[1,128]{1,0:T(1,128)S(1)}, f32[1,128]{1,0:T(1,128)S(1)}, u32[]{:S(2)}, u32[]{:S(2)}) %collective-permute-start.41) | collective-permute-done | bytes 544 | tf_op jit(solution)/shard_map/cond/branch_1_fun/ppermute | solution.py:312
  76.0 2.0 %collective-permute-done.36.refs_3_ = f32[3,16,1024]{2,1,0:T(8,128)S(1)} collective-permute-done((f32[3,16,1024]{2,1,0:T(8,128)S(1)}, f32[3,16,1024]{2,1,0:T(8,128)S(1)}, u32[]{:S(2)}, u32[]{:S(2)}) %collective-permute-start.36) | collective-permute-done | bytes 196640 | tf_op jit(solution)/shard_map/cond/branch_1_fun/ppermute | solution.py:312
  77.9 2.0 %place.13 = (f32[1,3,32,4096]{3,2,1,0:T(8,128)}, f32[1]{0:T(128)}) custom-call(s32[6]{0:T(128)S(1)} %get-tuple-element.117.at_ref, f32[3,16,1024]{2,1,0:T(8,128)S(1)} %get-tuple-element.145.refs_0_, f32[3,16,1024]{2,1,0:T(8,128)S(1)} %collective-permute-done.34.refs_1_, ...), custom_call_target="tpu_custom_call", output_to_operand_aliasing={{0}: (5, {})} | custom-call | tf_op jit(solution)/shard_map/cond/branch_1_fun/place/pallas_call | solution.py:224
  (46 shorter events, 11.5 us)
Async XLA Ops:
  0.6 3.3 %copy-start.5 = (f32[256]{0:T(256)S(1)}, f32[256]{0:T(256)}, u32[]{:S(2)}) copy-start(f32[256]{0:T(256)} %param.14) | copy-start | bytes 3076
  0.6 3.3 %copy-start.4 = (f32[256]{0:T(256)S(1)}, f32[256]{0:T(256)}, u32[]{:S(2)}) copy-start(f32[256]{0:T(256)} %param.13) | copy-start | bytes 3076
  0.7 3.3 %copy-start.3 = (s32[256]{0:T(256)S(1)}, s32[256]{0:T(256)}, u32[]{:S(2)}) copy-start(s32[256]{0:T(256)} %param.12) | copy-start | bytes 3076
  4.0 11.5 %collective-permute-start.21 = (f32[4,8,4096]{2,1,0:T(8,128)S(1)}, f32[4,8,4096]{2,1,0:T(8,128)S(1)}, u32[]{:S(2)}, u32[]{:S(2)}) collective-permute-start(f32[4,8,4096]{2,1,0:T(8,128)S(1)} %get-tuple-element.121), channel_id=1, source_target_pairs={{0,1},{1,2},{2,3},{4,5},{5,6},{6,7},{8,9},{9,10},{10,11},{12,13},{... | collective-permute-start | bytes 1572872 | tf_op jit(solution)/shard_map/cond/branch_1_fun/ppermute | solution.py:365
  6.4 9.1 %collective-permute-start.22 = (f32[4,8,4096]{2,1,0:T(8,128)S(1)}, f32[4,8,4096]{2,1,0:T(8,128)S(1)}, u32[]{:S(2)}, u32[]{:S(2)}) collective-permute-start(f32[4,8,4096]{2,1,0:T(8,128)S(1)} %get-tuple-element.122), channel_id=1, source_target_pairs={{1,0},{2,1},{3,2},{5,4},{6,5},{7,6},{9,8},{10,9},{11,10},{13,12},{... | collective-permute-start | bytes 1572872 | tf_op jit(solution)/shard_map/cond/branch_1_fun/ppermute | solution.py:366
  11.5 13.0 %collective-permute-start.26 = (f32[3,16,1024]{2,1,0:T(8,128)S(1)}, f32[3,16,1024]{2,1,0:T(8,128)S(1)}, u32[]{:S(2)}, u32[]{:S(2)}) collective-permute-start(f32[3,16,1024]{2,1,0:T(8,128)S(1)} %get-tuple-element.133), channel_id=1, source_target_pairs={{0,4},{4,0},{8,12},{12,8},{16,20},{20,16},{24,28},{28,24},{1,5},{5... | collective-permute-start | bytes 589832 | tf_op jit(solution)/shard_map/cond/branch_1_fun/ppermute | solution.py:312
  13.9 10.6 %collective-permute-start.27 = (f32[3,16,1024]{2,1,0:T(8,128)S(1)}, f32[3,16,1024]{2,1,0:T(8,128)S(1)}, u32[]{:S(2)}, u32[]{:S(2)}) collective-permute-start(f32[3,16,1024]{2,1,0:T(8,128)S(1)} %get-tuple-element.134), channel_id=1, source_target_pairs={{0,8},{4,12},{8,0},{12,4},{16,24},{20,28},{24,16},{28,20},{1,9},{5... | collective-permute-start | bytes 589832 | tf_op jit(solution)/shard_map/cond/branch_1_fun/ppermute | solution.py:312
  15.5 9.1 %collective-permute-start.28 = (f32[3,16,1024]{2,1,0:T(8,128)S(1)}, f32[3,16,1024]{2,1,0:T(8,128)S(1)}, u32[]{:S(2)}, u32[]{:S(2)}) collective-permute-start(f32[3,16,1024]{2,1,0:T(8,128)S(1)} %get-tuple-element.135), channel_id=1, source_target_pairs={{0,12},{4,8},{8,4},{12,0},{16,28},{20,24},{24,20},{28,16},{1,13},{... | collective-permute-start | bytes 589832 | tf_op jit(solution)/shard_map/cond/branch_1_fun/ppermute | solution.py:312
  21.0 26.0 %collective-permute-start.23 = (f32[3,16,1024]{2,1,0:T(8,128)S(1)}, f32[3,16,1024]{2,1,0:T(8,128)S(1)}, u32[]{:S(2)}, u32[]{:S(2)}) collective-permute-start(f32[3,16,1024]{2,1,0:T(8,128)S(1)} %get-tuple-element.124), channel_id=1, source_target_pairs={{0,4},{4,0},{8,12},{12,8},{16,20},{20,16},{24,28},{28,24},{1,5},{5... | collective-permute-start | bytes 589832 | tf_op jit(solution)/shard_map/cond/branch_1_fun/ppermute | solution.py:312
  23.0 24.0 %collective-permute-start.24 = (f32[3,16,1024]{2,1,0:T(8,128)S(1)}, f32[3,16,1024]{2,1,0:T(8,128)S(1)}, u32[]{:S(2)}, u32[]{:S(2)}) collective-permute-start(f32[3,16,1024]{2,1,0:T(8,128)S(1)} %get-tuple-element.125), channel_id=1, source_target_pairs={{0,8},{4,12},{8,0},{12,4},{16,24},{20,28},{24,16},{28,20},{1,9},{5... | collective-permute-start | bytes 589832 | tf_op jit(solution)/shard_map/cond/branch_1_fun/ppermute | solution.py:312
  24.6 22.4 %collective-permute-start.25 = (f32[3,16,1024]{2,1,0:T(8,128)S(1)}, f32[3,16,1024]{2,1,0:T(8,128)S(1)}, u32[]{:S(2)}, u32[]{:S(2)}) collective-permute-start(f32[3,16,1024]{2,1,0:T(8,128)S(1)} %get-tuple-element.126), channel_id=1, source_target_pairs={{0,12},{4,8},{8,4},{12,0},{16,28},{20,24},{24,20},{28,16},{1,13},{... | collective-permute-start | bytes 589832 | tf_op jit(solution)/shard_map/cond/branch_1_fun/ppermute | solution.py:312
  25.2 22.8 %collective-permute-start.37 = (f32[2,3,16,1024]{3,2,1,0:T(8,128)S(1)}, f32[2,3,16,1024]{3,2,1,0:T(8,128)S(1)}, u32[]{:S(2)}, u32[]{:S(2)}) collective-permute-start(f32[2,3,16,1024]{3,2,1,0:T(8,128)S(1)} %pick.24), channel_id=1, source_target_pairs={{0,16},{4,20},{8,24},{12,28},{16,0},{20,4},{24,8},{28,12},{1,17},{... | collective-permute-start | bytes 1179656 | tf_op jit(solution)/shard_map/cond/branch_1_fun/ppermute | solution.py:312
  32.7 3.6 %collective-permute-start.29 = (f32[1,128]{1,0:T(1,128)S(1)}, f32[1,128]{1,0:T(1,128)S(1)}, u32[]{:S(2)}, u32[]{:S(2)}) collective-permute-start(f32[1,128]{1,0:T(1,128)S(1)} %misfit.5), channel_id=1, source_target_pairs={{0,1},{1,0},{2,3},{3,2},{4,5},{5,4},{6,7},{7,6},{8,9},{9,8},{10,11... | collective-permute-start | bytes 1544 | tf_op jit(solution)/shard_map/cond/branch_1_fun/ppermute | solution.py:164
  36.3 3.5 %collective-permute-start.30 = (f32[1,128]{1,0:T(1,128)S(1)}, f32[1,128]{1,0:T(1,128)S(1)}, u32[]{:S(2)}, u32[]{:S(2)}) collective-permute-start(f32[1,128]{1,0:T(1,128)S(1)} %add.42), channel_id=1, source_target_pairs={{0,2},{1,3},{2,0},{3,1},{4,6},{5,7},{6,4},{7,5},{8,10},{9,11},{10,... | collective-permute-start | bytes 1544 | tf_op jit(solution)/shard_map/cond/branch_1_fun/ppermute | solution.py:164
  39.9 3.5 %collective-permute-start.31 = (f32[1,128]{1,0:T(1,128)S(1)}, f32[1,128]{1,0:T(1,128)S(1)}, u32[]{:S(2)}, u32[]{:S(2)}) collective-permute-start(f32[1,128]{1,0:T(1,128)S(1)} %add.43), channel_id=1, source_target_pairs={{0,4},{4,0},{8,12},{12,8},{16,20},{20,16},{24,28},{28,24},{1,5},{5... | collective-permute-start | bytes 1544 | tf_op jit(solution)/shard_map/cond/branch_1_fun/ppermute | solution.py:312
  43.4 3.5 %collective-permute-start.32 = (f32[1,128]{1,0:T(1,128)S(1)}, f32[1,128]{1,0:T(1,128)S(1)}, u32[]{:S(2)}, u32[]{:S(2)}) collective-permute-start(f32[1,128]{1,0:T(1,128)S(1)} %add.44), channel_id=1, source_target_pairs={{0,8},{4,12},{8,0},{12,4},{16,24},{20,28},{24,16},{28,20},{1,9},{5... | collective-permute-start | bytes 1544 | tf_op jit(solution)/shard_map/cond/branch_1_fun/ppermute | solution.py:312
  47.6 17.8 %collective-permute-start.33 = (f32[2,3,16,1024]{3,2,1,0:T(8,128)S(1)}, f32[2,3,16,1024]{3,2,1,0:T(8,128)S(1)}, u32[]{:S(2)}, u32[]{:S(2)}) collective-permute-start(f32[2,3,16,1024]{3,2,1,0:T(8,128)S(1)} %pick.25), channel_id=1, source_target_pairs={{0,16},{4,20},{8,24},{12,28},{16,0},{20,4},{24,8},{28,12},{1,17},{... | collective-permute-start | bytes 1179656 | tf_op jit(solution)/shard_map/cond/branch_1_fun/ppermute | solution.py:312
  48.7 19.4 %collective-permute-start.38 = (f32[3,16,1024]{2,1,0:T(8,128)S(1)}, f32[3,16,1024]{2,1,0:T(8,128)S(1)}, u32[]{:S(2)}, u32[]{:S(2)}) collective-permute-start(f32[3,16,1024]{2,1,0:T(8,128)S(1)} %get-tuple-element.151), channel_id=1, source_target_pairs={{0,4},{4,0},{8,12},{12,8},{16,20},{20,16},{24,28},{28,24},{1,5},{5... | collective-permute-start | bytes 589832 | tf_op jit(solution)/shard_map/cond/branch_1_fun/ppermute | solution.py:312
  50.1 19.5 %collective-permute-start.39 = (f32[3,16,1024]{2,1,0:T(8,128)S(1)}, f32[3,16,1024]{2,1,0:T(8,128)S(1)}, u32[]{:S(2)}, u32[]{:S(2)}) collective-permute-start(f32[3,16,1024]{2,1,0:T(8,128)S(1)} %get-tuple-element.152), channel_id=1, source_target_pairs={{0,8},{4,12},{8,0},{12,4},{16,24},{20,28},{24,16},{28,20},{1,9},{5... | collective-permute-start | bytes 589832 | tf_op jit(solution)/shard_map/cond/branch_1_fun/ppermute | solution.py:312
  51.7 18.6 %collective-permute-start.40 = (f32[3,16,1024]{2,1,0:T(8,128)S(1)}, f32[3,16,1024]{2,1,0:T(8,128)S(1)}, u32[]{:S(2)}, u32[]{:S(2)}) collective-permute-start(f32[3,16,1024]{2,1,0:T(8,128)S(1)} %get-tuple-element.153), channel_id=1, source_target_pairs={{0,12},{4,8},{8,4},{12,0},{16,28},{20,24},{24,20},{28,16},{1,13},{... | collective-permute-start | bytes 589832 | tf_op jit(solution)/shard_map/cond/branch_1_fun/ppermute | solution.py:312
  66.1 9.9 %collective-permute-start.34 = (f32[3,16,1024]{2,1,0:T(8,128)S(1)}, f32[3,16,1024]{2,1,0:T(8,128)S(1)}, u32[]{:S(2)}, u32[]{:S(2)}) collective-permute-start(f32[3,16,1024]{2,1,0:T(8,128)S(1)} %get-tuple-element.146), channel_id=1, source_target_pairs={{0,4},{4,0},{8,12},{12,8},{16,20},{20,16},{24,28},{28,24},{1,5},{5... | collective-permute-start | bytes 589832 | tf_op jit(solution)/shard_map/cond/branch_1_fun/ppermute | solution.py:312
  68.1 7.9 %collective-permute-start.35 = (f32[3,16,1024]{2,1,0:T(8,128)S(1)}, f32[3,16,1024]{2,1,0:T(8,128)S(1)}, u32[]{:S(2)}, u32[]{:S(2)}) collective-permute-start(f32[3,16,1024]{2,1,0:T(8,128)S(1)} %get-tuple-element.147), channel_id=1, source_target_pairs={{0,8},{4,12},{8,0},{12,4},{16,24},{20,28},{24,16},{28,20},{1,9},{5... | collective-permute-start | bytes 589832 | tf_op jit(solution)/shard_map/cond/branch_1_fun/ppermute | solution.py:312
  68.1 9.9 %collective-permute-start.36 = (f32[3,16,1024]{2,1,0:T(8,128)S(1)}, f32[3,16,1024]{2,1,0:T(8,128)S(1)}, u32[]{:S(2)}, u32[]{:S(2)}) collective-permute-start(f32[3,16,1024]{2,1,0:T(8,128)S(1)} %get-tuple-element.148), channel_id=1, source_target_pairs={{0,12},{4,8},{8,4},{12,0},{16,28},{20,24},{24,20},{28,16},{1,13},{... | collective-permute-start | bytes 589832 | tf_op jit(solution)/shard_map/cond/branch_1_fun/ppermute | solution.py:312
  69.6 6.4 %collective-permute-start.41 = (f32[1,128]{1,0:T(1,128)S(1)}, f32[1,128]{1,0:T(1,128)S(1)}, u32[]{:S(2)}, u32[]{:S(2)}) collective-permute-start(f32[1,128]{1,0:T(1,128)S(1)} %add.45.refs_5_), channel_id=1, source_target_pairs={{0,16},{4,20},{8,24},{12,28},{16,0},{20,4},{24,8},{28,12},{1,17},{... | collective-permute-start | bytes 1544 | tf_op jit(solution)/shard_map/cond/branch_1_fun/ppermute | solution.py:312
  (3 other events, 5.8 us)

commit v2 on v1

--- a/solution.py
+++ b/solution.py
@@ -305,7 +305,7 @@
         scratch_shapes=[pltpu.SMEM(parent_lookup.shape, jnp.int32), pltpu.SemaphoreType.DMA((5,))],
         compiler_params=pltpu.CompilerParams(vmem_limit_bytes=VMEM_BYTES),
         name="prepare",
-    )(at, parent_lookup, fields, depth)
+    )(at, pltpu.with_memory_space_constraint(parent_lookup, pltpu.HBM), fields, depth)
 
 
 def to_mate(x, m):

time: 80.5 us -> 80 us (level)
  no operation moved by 1% of the time
where the time goes in v2:
time: 80 us; the launch traced here: 79.9 us
  starting transfers between devices  29.8 us (37%)
  waiting for transfers between devices  26.5 us (33%)
  Pallas kernels  22.1 us (28%)
  between operations  0.98 us (1%)
    ppermute x17, waiting for transfers between devices, to_mate(): lax.ppermute(x, 'dom', [(i, i ^ m) for i in range(lax.axis_size('dom'))])  23.4 us
    ppermute x17, starting transfers between devices, to_mate(): lax.ppermute(x, 'dom', [(i, i ^ m) for i in range(lax.axis_size('dom'))])  21.8 us
    pallas_call x2, Pallas kernels, forecast(): pl.pallas_call(kernel, out_shape=[jax.ShapeDtypeStruct(shape, jnp.float32...  9.26 us
    pallas_call x1, Pallas kernels, misfit(): pl.pallas_call(misfit_kernel, out_shape=jax.ShapeDtypeStruct((1, LANES),...  4.37 us
    ppermute x2, starting transfers between devices, sum_over(): x = x + lax.ppermute(x, axis, [(i, i ^ step) for i in range(count)])  4.32 us
    pallas_call x2, Pallas kernels, place(): pl.pallas_call(kernel, out_shape=out_shape, in_specs=[in_smem] + [in_vmem...  3.44 us
    ppermute x2, waiting for transfers between devices, sum_over(): x = x + lax.ppermute(x, axis, [(i, i ^ step) for i in range(count)])  3.04 us
    pallas_call x4, Pallas kernels, pick(): pl.pallas_call(kernel, out_shape=[jax.ShapeDtypeStruct(shape, jnp.float32...  2.61 us
  transfers between devices with their start and end apart: 21, of which 7 were waited for; matrix products, arithmetic and copies ran while one was open for 0% of the time, Pallas kernels for 22%

profile of v2, /device:TPU:0, one launch (start us, length us, event | category | flops | bytes accessed | tf_op | source)
XLA Modules:
  0.0 79.9 jit_solution(16965833148579999863)
XLA Ops:
  0.8 2.4 %prepare.1 = (s32[9]{0:T(128)S(1)}, f32[4,8,4096]{2,1,0:T(8,128)S(1)}, f32[4,8,4096]{2,1,0:T(8,128)S(1)}) custom-call(s32[6]{0:T(128)S(1)} %stack.35.refs_0_, s32[8]{0:T(128)} %refs_1_.1, f32[1,3,32,4096]{3,2,1,0:T(8,128)} %refs_2_.1, f32[32,4096]{1,0:T(8,128)} %refs_3_.1), custom_call_target="tpu_custom_call" | custom-call | tf_op jit(solution)/shard_map/prepare/pallas_call | solution.py:300
  3.3 76.4 %conditional.1 = (f32[1]{0:T(128)}, f32[1,3,32,4096]{3,2,1,0:T(8,128)}) conditional(s32[]{:T(128)} %bitcast.6, (f32[4,8,4096]{2,1,0:T(8,128)S(1)}, f32[4,8,4096]{2,1,0:T(8,128)S(1)}, s32[6]{0:T(128)S(1)}, f32[1,3,32,4096]{3,2,1,0:T(8,128)S(1)}, f32[32,4096]{1,0:T(8,128)S(1)}, /*index=5*/s32[9]{0:T(128)S(1)}, ...), branch_computations={%region_0.1_spmd, %region_1.2_spmd, %region_2.3_spmd, %region_3.4_... | conditional | flops 512 | bytes 19940344 | solution.py:434
  3.3 2.4 %collective-permute-start.21 = (f32[4,8,4096]{2,1,0:T(8,128)S(1)}, f32[4,8,4096]{2,1,0:T(8,128)S(1)}, u32[]{:S(2)}, u32[]{:S(2)}) collective-permute-start(f32[4,8,4096]{2,1,0:T(8,128)S(1)} %get-tuple-element.121), channel_id=1, source_target_pairs={{0,1},{1,2},{2,3},{4,5},{5,6},{6,7},{8,9},{9,10},{10,11},{12,13},{... | collective-permute-start | bytes 1572872 | tf_op jit(solution)/shard_map/cond/branch_1_fun/ppermute | solution.py:365
  7.0 3.8 %inner.5 = (f32[3,16,1024]{2,1,0:T(8,128)S(1)}, f32[3,16,1024]{2,1,0:T(8,128)S(1)}, f32[3,16,1024]{2,1,0:T(8,128)S(1)}, f32[3,16,1024]{2,1,0:T(8,128)S(1)}, f32[16,4096]{1,0:T(8,128)S(1)}) custom-call(s32[6]{0:T(128)S(1)} %get-tuple-element.117.at_ref, f32[1,3,32,4096]{3,2,1,0:T(8,128)S(1)} %get-tuple-element.119.fields_ref, ...), custom_call_target="tpu_custom_call" | custom-call | tf_op jit(solution)/shard_map/cond/branch_1_fun/inner/pallas_call | solution.py:93
  10.8 2.4 %collective-permute-start.26 = (f32[3,16,1024]{2,1,0:T(8,128)S(1)}, f32[3,16,1024]{2,1,0:T(8,128)S(1)}, u32[]{:S(2)}, u32[]{:S(2)}) collective-permute-start(f32[3,16,1024]{2,1,0:T(8,128)S(1)} %get-tuple-element.133), channel_id=1, source_target_pairs={{0,4},{4,0},{8,12},{12,8},{16,20},{20,16},{24,28},{28,24},{1,5},{5... | collective-permute-start | bytes 589832 | tf_op jit(solution)/shard_map/cond/branch_1_fun/ppermute | solution.py:312
  13.2 1.6 %collective-permute-start.27 = (f32[3,16,1024]{2,1,0:T(8,128)S(1)}, f32[3,16,1024]{2,1,0:T(8,128)S(1)}, u32[]{:S(2)}, u32[]{:S(2)}) collective-permute-start(f32[3,16,1024]{2,1,0:T(8,128)S(1)} %get-tuple-element.134), channel_id=1, source_target_pairs={{0,8},{4,12},{8,0},{12,4},{16,24},{20,28},{24,16},{28,20},{1,9},{5... | collective-permute-start | bytes 589832 | tf_op jit(solution)/shard_map/cond/branch_1_fun/ppermute | solution.py:312
  14.8 5.5 %outer.5 = (f32[3,16,1024]{2,1,0:T(8,128)S(1)}, f32[3,16,1024]{2,1,0:T(8,128)S(1)}, f32[3,16,1024]{2,1,0:T(8,128)S(1)}, f32[3,16,1024]{2,1,0:T(8,128)S(1)}, f32[16,4096]{1,0:T(8,128)S(1)}) custom-call(s32[6]{0:T(128)S(1)} %get-tuple-element.117.at_ref, f32[1,3,32,4096]{3,2,1,0:T(8,128)S(1)} %get-tuple-element.119.fields_ref, ...), custom_call_target="tpu_custom_call" | custom-call | tf_op jit(solution)/shard_map/cond/branch_1_fun/outer/pallas_call | solution.py:93
  20.3 2.0 %collective-permute-start.23 = (f32[3,16,1024]{2,1,0:T(8,128)S(1)}, f32[3,16,1024]{2,1,0:T(8,128)S(1)}, u32[]{:S(2)}, u32[]{:S(2)}) collective-permute-start(f32[3,16,1024]{2,1,0:T(8,128)S(1)} %get-tuple-element.124), channel_id=1, source_target_pairs={{0,4},{4,0},{8,12},{12,8},{16,20},{20,16},{24,28},{28,24},{1,5},{5... | collective-permute-start | bytes 589832 | tf_op jit(solution)/shard_map/cond/branch_1_fun/ppermute | solution.py:312
  22.2 1.6 %collective-permute-start.24 = (f32[3,16,1024]{2,1,0:T(8,128)S(1)}, f32[3,16,1024]{2,1,0:T(8,128)S(1)}, u32[]{:S(2)}, u32[]{:S(2)}) collective-permute-start(f32[3,16,1024]{2,1,0:T(8,128)S(1)} %get-tuple-element.125), channel_id=1, source_target_pairs={{0,8},{4,12},{8,0},{12,4},{16,24},{20,28},{24,16},{28,20},{1,9},{5... | collective-permute-start | bytes 589832 | tf_op jit(solution)/shard_map/cond/branch_1_fun/ppermute | solution.py:312
  24.5 3.0 %collective-permute-start.37 = (f32[2,3,16,1024]{3,2,1,0:T(8,128)S(1)}, f32[2,3,16,1024]{3,2,1,0:T(8,128)S(1)}, u32[]{:S(2)}, u32[]{:S(2)}) collective-permute-start(f32[2,3,16,1024]{3,2,1,0:T(8,128)S(1)} %pick.24), channel_id=1, source_target_pairs={{0,16},{4,20},{8,24},{12,28},{16,0},{20,4},{24,8},{28,12},{1,17},{... | collective-permute-start | bytes 1179656 | tf_op jit(solution)/shard_map/cond/branch_1_fun/ppermute | solution.py:312
  27.5 4.4 %misfit.5 = f32[1,128]{1,0:T(1,128)S(1)} custom-call(s32[6]{0:T(128)S(1)} %get-tuple-element.117.at_ref, s32[256]{0:T(256)S(1)} %get-tuple-element.127.index_ref, f32[256]{0:T(256)S(1)} %get-tuple-element.128.value_ref, f32[256]{0:T(256)S(1)} %get-tuple-element.129.var_ref, f32[16,4096]{1,0:T(8,128)S(1)} %get-tuple-element.130.inner_ref, ...), custom_call_target="tpu_custom_call" | custom-call | tf_op jit(solution)/shard_map/cond/branch_1_fun/misfit/pallas_call | solution.py:149
  31.9 3.0 %collective-permute-start.29 = (f32[1,128]{1,0:T(1,128)S(1)}, f32[1,128]{1,0:T(1,128)S(1)}, u32[]{:S(2)}, u32[]{:S(2)}) collective-permute-start(f32[1,128]{1,0:T(1,128)S(1)} %misfit.5), channel_id=1, source_target_pairs={{0,1},{1,0},{2,3},{3,2},{4,5},{5,4},{6,7},{7,6},{8,9},{9,8},{10,11... | collective-permute-start | bytes 1544 | tf_op jit(solution)/shard_map/cond/branch_1_fun/ppermute | solution.py:164
  37.0 2.2 %collective-permute-done.30 = f32[1,128]{1,0:T(1,128)S(1)} collective-permute-done((f32[1,128]{1,0:T(1,128)S(1)}, f32[1,128]{1,0:T(1,128)S(1)}, u32[]{:S(2)}, u32[]{:S(2)}) %collective-permute-start.30) | collective-permute-done | bytes 544 | tf_op jit(solution)/shard_map/cond/branch_1_fun/ppermute | solution.py:164
  40.6 2.1 %collective-permute-done.31 = f32[1,128]{1,0:T(1,128)S(1)} collective-permute-done((f32[1,128]{1,0:T(1,128)S(1)}, f32[1,128]{1,0:T(1,128)S(1)}, u32[]{:S(2)}, u32[]{:S(2)}) %collective-permute-start.31) | collective-permute-done | bytes 544 | tf_op jit(solution)/shard_map/cond/branch_1_fun/ppermute | solution.py:312
  42.8 1.6 %collective-permute-start.32 = (f32[1,128]{1,0:T(1,128)S(1)}, f32[1,128]{1,0:T(1,128)S(1)}, u32[]{:S(2)}, u32[]{:S(2)}) collective-permute-start(f32[1,128]{1,0:T(1,128)S(1)} %add.44), channel_id=1, source_target_pairs={{0,8},{4,12},{8,0},{12,4},{16,24},{20,28},{24,16},{28,20},{1,9},{5... | collective-permute-start | bytes 1544 | tf_op jit(solution)/shard_map/cond/branch_1_fun/ppermute | solution.py:312
  44.4 2.0 %collective-permute-done.32 = f32[1,128]{1,0:T(1,128)S(1)} collective-permute-done((f32[1,128]{1,0:T(1,128)S(1)}, f32[1,128]{1,0:T(1,128)S(1)}, u32[]{:S(2)}, u32[]{:S(2)}) %collective-permute-start.32) | collective-permute-done | bytes 544 | tf_op jit(solution)/shard_map/cond/branch_1_fun/ppermute | solution.py:312
  49.5 1.6 %collective-permute-start.39 = (f32[3,16,1024]{2,1,0:T(8,128)S(1)}, f32[3,16,1024]{2,1,0:T(8,128)S(1)}, u32[]{:S(2)}, u32[]{:S(2)}) collective-permute-start(f32[3,16,1024]{2,1,0:T(8,128)S(1)} %get-tuple-element.152), channel_id=1, source_target_pairs={{0,8},{4,12},{8,0},{12,4},{16,24},{20,28},{24,16},{28,20},{1,9},{5... | collective-permute-start | bytes 589832 | tf_op jit(solution)/shard_map/cond/branch_1_fun/ppermute | solution.py:312
  51.6 13.0 %collective-permute-done.33.refs_4_ = f32[2,3,16,1024]{3,2,1,0:T(8,128)S(1)} collective-permute-done((f32[2,3,16,1024]{3,2,1,0:T(8,128)S(1)}, f32[2,3,16,1024]{3,2,1,0:T(8,128)S(1)}, u32[]{:S(2)}, u32[]{:S(2)}) %collective-permute-start.33) | collective-permute-done | bytes 393248 | tf_op jit(solution)/shard_map/cond/branch_1_fun/ppermute | solution.py:312
  65.3 2.1 %collective-permute-start.34 = (f32[3,16,1024]{2,1,0:T(8,128)S(1)}, f32[3,16,1024]{2,1,0:T(8,128)S(1)}, u32[]{:S(2)}, u32[]{:S(2)}) collective-permute-start(f32[3,16,1024]{2,1,0:T(8,128)S(1)} %get-tuple-element.146), channel_id=1, source_target_pairs={{0,4},{4,0},{8,12},{12,8},{16,20},{20,16},{24,28},{28,24},{1,5},{5... | collective-permute-start | bytes 589832 | tf_op jit(solution)/shard_map/cond/branch_1_fun/ppermute | solution.py:312
  67.5 1.5 %collective-permute-start.36 = (f32[3,16,1024]{2,1,0:T(8,128)S(1)}, f32[3,16,1024]{2,1,0:T(8,128)S(1)}, u32[]{:S(2)}, u32[]{:S(2)}) collective-permute-start(f32[3,16,1024]{2,1,0:T(8,128)S(1)} %get-tuple-element.148), channel_id=1, source_target_pairs={{0,12},{4,8},{8,4},{12,0},{16,28},{20,24},{24,20},{28,16},{1,13},{... | collective-permute-start | bytes 589832 | tf_op jit(solution)/shard_map/cond/branch_1_fun/ppermute | solution.py:312
  69.7 1.4 %place.12.refs_4_ = f32[1,3,32,4096]{3,2,1,0:T(8,128)} custom-call(s32[6]{0:T(128)S(1)} %get-tuple-element.117.at_ref, f32[3,16,1024]{2,1,0:T(8,128)S(1)} %get-tuple-element.154.refs_0_, f32[3,16,1024]{2,1,0:T(8,128)S(1)} %collective-permute-done.38.refs_1_, f32[3,16,1024]{2,1,0:T(8,128)S(1)} %collective-permute-done.39.refs_2_, ...), custom_call_target="tpu_custom_call" | custom-call | tf_op jit(solution)/shard_map/cond/branch_1_fun/place/pallas_call | solution.py:224
  71.1 4.3 %collective-permute-done.41.refs_6_ = f32[1,128]{1,0:T(1,128)S(1)} collective-permute-done((f32[1,128]{1,0:T(1,128)S(1)}, f32[1,128]{1,0:T(1,128)S(1)}, u32[]{:S(2)}, u32[]{:S(2)}) %collective-permute-start.41) | collective-permute-done | bytes 544 | tf_op jit(solution)/shard_map/cond/branch_1_fun/ppermute | solution.py:312
  75.5 2.0 %collective-permute-done.36.refs_3_ = f32[3,16,1024]{2,1,0:T(8,128)S(1)} collective-permute-done((f32[3,16,1024]{2,1,0:T(8,128)S(1)}, f32[3,16,1024]{2,1,0:T(8,128)S(1)}, u32[]{:S(2)}, u32[]{:S(2)}) %collective-permute-start.36) | collective-permute-done | bytes 196640 | tf_op jit(solution)/shard_map/cond/branch_1_fun/ppermute | solution.py:312
  77.4 2.0 %place.13 = (f32[1,3,32,4096]{3,2,1,0:T(8,128)}, f32[1]{0:T(128)}) custom-call(s32[6]{0:T(128)S(1)} %get-tuple-element.117.at_ref, f32[3,16,1024]{2,1,0:T(8,128)S(1)} %get-tuple-element.145.refs_0_, f32[3,16,1024]{2,1,0:T(8,128)S(1)} %collective-permute-done.34.refs_1_, ...), custom_call_target="tpu_custom_call", output_to_operand_aliasing={{0}: (5, {})} | custom-call | tf_op jit(solution)/shard_map/cond/branch_1_fun/place/pallas_call | solution.py:224
  (44 shorter events, 10.6 us)
Async XLA Ops:
  0.6 2.6 %copy-start.1 = (f32[32,4096]{1,0:T(8,128)S(1)}, f32[32,4096]{1,0:T(8,128)}, u32[]{:S(2)}) copy-start(f32[32,4096]{1,0:T(8,128)} %refs_3_.1) | copy-start | bytes 1572868
  0.6 2.6 %copy-start = (f32[1,3,32,4096]{3,2,1,0:T(8,128)S(1)}, f32[1,3,32,4096]{3,2,1,0:T(8,128)}, u32[]{:S(2)}) copy-start(f32[1,3,32,4096]{3,2,1,0:T(8,128)} %refs_2_.1) | copy-start | bytes 4718596
  0.7 2.6 %copy-start.4 = (f32[256]{0:T(256)S(1)}, f32[256]{0:T(256)}, u32[]{:S(2)}) copy-start(f32[256]{0:T(256)} %param.14) | copy-start | bytes 3076
  3.3 11.5 %collective-permute-start.21 = (f32[4,8,4096]{2,1,0:T(8,128)S(1)}, f32[4,8,4096]{2,1,0:T(8,128)S(1)}, u32[]{:S(2)}, u32[]{:S(2)}) collective-permute-start(f32[4,8,4096]{2,1,0:T(8,128)S(1)} %get-tuple-element.121), channel_id=1, source_target_pairs={{0,1},{1,2},{2,3},{4,5},{5,6},{6,7},{8,9},{9,10},{10,11},{12,13},{... | collective-permute-start | bytes 1572872 | tf_op jit(solution)/shard_map/cond/branch_1_fun/ppermute | solution.py:365
  5.7 9.1 %collective-permute-start.22 = (f32[4,8,4096]{2,1,0:T(8,128)S(1)}, f32[4,8,4096]{2,1,0:T(8,128)S(1)}, u32[]{:S(2)}, u32[]{:S(2)}) collective-permute-start(f32[4,8,4096]{2,1,0:T(8,128)S(1)} %get-tuple-element.122), channel_id=1, source_target_pairs={{1,0},{2,1},{3,2},{5,4},{6,5},{7,6},{9,8},{10,9},{11,10},{13,12},{... | collective-permute-start | bytes 1572872 | tf_op jit(solution)/shard_map/cond/branch_1_fun/ppermute | solution.py:366
  10.8 13.0 %collective-permute-start.26 = (f32[3,16,1024]{2,1,0:T(8,128)S(1)}, f32[3,16,1024]{2,1,0:T(8,128)S(1)}, u32[]{:S(2)}, u32[]{:S(2)}) collective-permute-start(f32[3,16,1024]{2,1,0:T(8,128)S(1)} %get-tuple-element.133), channel_id=1, source_target_pairs={{0,4},{4,0},{8,12},{12,8},{16,20},{20,16},{24,28},{28,24},{1,5},{5... | collective-permute-start | bytes 589832 | tf_op jit(solution)/shard_map/cond/branch_1_fun/ppermute | solution.py:312
  13.2 10.6 %collective-permute-start.27 = (f32[3,16,1024]{2,1,0:T(8,128)S(1)}, f32[3,16,1024]{2,1,0:T(8,128)S(1)}, u32[]{:S(2)}, u32[]{:S(2)}) collective-permute-start(f32[3,16,1024]{2,1,0:T(8,128)S(1)} %get-tuple-element.134), channel_id=1, source_target_pairs={{0,8},{4,12},{8,0},{12,4},{16,24},{20,28},{24,16},{28,20},{1,9},{5... | collective-permute-start | bytes 589832 | tf_op jit(solution)/shard_map/cond/branch_1_fun/ppermute | solution.py:312
  14.8 9.1 %collective-permute-start.28 = (f32[3,16,1024]{2,1,0:T(8,128)S(1)}, f32[3,16,1024]{2,1,0:T(8,128)S(1)}, u32[]{:S(2)}, u32[]{:S(2)}) collective-permute-start(f32[3,16,1024]{2,1,0:T(8,128)S(1)} %get-tuple-element.135), channel_id=1, source_target_pairs={{0,12},{4,8},{8,4},{12,0},{16,28},{20,24},{24,20},{28,16},{1,13},{... | collective-permute-start | bytes 589832 | tf_op jit(solution)/shard_map/cond/branch_1_fun/ppermute | solution.py:312
  20.3 26.1 %collective-permute-start.23 = (f32[3,16,1024]{2,1,0:T(8,128)S(1)}, f32[3,16,1024]{2,1,0:T(8,128)S(1)}, u32[]{:S(2)}, u32[]{:S(2)}) collective-permute-start(f32[3,16,1024]{2,1,0:T(8,128)S(1)} %get-tuple-element.124), channel_id=1, source_target_pairs={{0,4},{4,0},{8,12},{12,8},{16,20},{20,16},{24,28},{28,24},{1,5},{5... | collective-permute-start | bytes 589832 | tf_op jit(solution)/shard_map/cond/branch_1_fun/ppermute | solution.py:312
  22.2 24.1 %collective-permute-start.24 = (f32[3,16,1024]{2,1,0:T(8,128)S(1)}, f32[3,16,1024]{2,1,0:T(8,128)S(1)}, u32[]{:S(2)}, u32[]{:S(2)}) collective-permute-start(f32[3,16,1024]{2,1,0:T(8,128)S(1)} %get-tuple-element.125), channel_id=1, source_target_pairs={{0,8},{4,12},{8,0},{12,4},{16,24},{20,28},{24,16},{28,20},{1,9},{5... | collective-permute-start | bytes 589832 | tf_op jit(solution)/shard_map/cond/branch_1_fun/ppermute | solution.py:312
  23.8 22.5 %collective-permute-start.25 = (f32[3,16,1024]{2,1,0:T(8,128)S(1)}, f32[3,16,1024]{2,1,0:T(8,128)S(1)}, u32[]{:S(2)}, u32[]{:S(2)}) collective-permute-start(f32[3,16,1024]{2,1,0:T(8,128)S(1)} %get-tuple-element.126), channel_id=1, source_target_pairs={{0,12},{4,8},{8,4},{12,0},{16,28},{20,24},{24,20},{28,16},{1,13},{... | collective-permute-start | bytes 589832 | tf_op jit(solution)/shard_map/cond/branch_1_fun/ppermute | solution.py:312
  24.5 22.9 %collective-permute-start.37 = (f32[2,3,16,1024]{3,2,1,0:T(8,128)S(1)}, f32[2,3,16,1024]{3,2,1,0:T(8,128)S(1)}, u32[]{:S(2)}, u32[]{:S(2)}) collective-permute-start(f32[2,3,16,1024]{3,2,1,0:T(8,128)S(1)} %pick.24), channel_id=1, source_target_pairs={{0,16},{4,20},{8,24},{12,28},{16,0},{20,4},{24,8},{28,12},{1,17},{... | collective-permute-start | bytes 1179656 | tf_op jit(solution)/shard_map/cond/branch_1_fun/ppermute | solution.py:312
  31.9 3.8 %collective-permute-start.29 = (f32[1,128]{1,0:T(1,128)S(1)}, f32[1,128]{1,0:T(1,128)S(1)}, u32[]{:S(2)}, u32[]{:S(2)}) collective-permute-start(f32[1,128]{1,0:T(1,128)S(1)} %misfit.5), channel_id=1, source_target_pairs={{0,1},{1,0},{2,3},{3,2},{4,5},{5,4},{6,7},{7,6},{8,9},{9,8},{10,11... | collective-permute-start | bytes 1544 | tf_op jit(solution)/shard_map/cond/branch_1_fun/ppermute | solution.py:164
  35.7 3.5 %collective-permute-start.30 = (f32[1,128]{1,0:T(1,128)S(1)}, f32[1,128]{1,0:T(1,128)S(1)}, u32[]{:S(2)}, u32[]{:S(2)}) collective-permute-start(f32[1,128]{1,0:T(1,128)S(1)} %add.42), channel_id=1, source_target_pairs={{0,2},{1,3},{2,0},{3,1},{4,6},{5,7},{6,4},{7,5},{8,10},{9,11},{10,... | collective-permute-start | bytes 1544 | tf_op jit(solution)/shard_map/cond/branch_1_fun/ppermute | solution.py:164
  39.2 3.5 %collective-permute-start.31 = (f32[1,128]{1,0:T(1,128)S(1)}, f32[1,128]{1,0:T(1,128)S(1)}, u32[]{:S(2)}, u32[]{:S(2)}) collective-permute-start(f32[1,128]{1,0:T(1,128)S(1)} %add.43), channel_id=1, source_target_pairs={{0,4},{4,0},{8,12},{12,8},{16,20},{20,16},{24,28},{28,24},{1,5},{5... | collective-permute-start | bytes 1544 | tf_op jit(solution)/shard_map/cond/branch_1_fun/ppermute | solution.py:312
  42.8 3.5 %collective-permute-start.32 = (f32[1,128]{1,0:T(1,128)S(1)}, f32[1,128]{1,0:T(1,128)S(1)}, u32[]{:S(2)}, u32[]{:S(2)}) collective-permute-start(f32[1,128]{1,0:T(1,128)S(1)} %add.44), channel_id=1, source_target_pairs={{0,8},{4,12},{8,0},{12,4},{16,24},{20,28},{24,16},{28,20},{1,9},{5... | collective-permute-start | bytes 1544 | tf_op jit(solution)/shard_map/cond/branch_1_fun/ppermute | solution.py:312
  47.0 17.7 %collective-permute-start.33 = (f32[2,3,16,1024]{3,2,1,0:T(8,128)S(1)}, f32[2,3,16,1024]{3,2,1,0:T(8,128)S(1)}, u32[]{:S(2)}, u32[]{:S(2)}) collective-permute-start(f32[2,3,16,1024]{3,2,1,0:T(8,128)S(1)} %pick.25), channel_id=1, source_target_pairs={{0,16},{4,20},{8,24},{12,28},{16,0},{20,4},{24,8},{28,12},{1,17},{... | collective-permute-start | bytes 1179656 | tf_op jit(solution)/shard_map/cond/branch_1_fun/ppermute | solution.py:312
  48.1 19.4 %collective-permute-start.38 = (f32[3,16,1024]{2,1,0:T(8,128)S(1)}, f32[3,16,1024]{2,1,0:T(8,128)S(1)}, u32[]{:S(2)}, u32[]{:S(2)}) collective-permute-start(f32[3,16,1024]{2,1,0:T(8,128)S(1)} %get-tuple-element.151), channel_id=1, source_target_pairs={{0,4},{4,0},{8,12},{12,8},{16,20},{20,16},{24,28},{28,24},{1,5},{5... | collective-permute-start | bytes 589832 | tf_op jit(solution)/shard_map/cond/branch_1_fun/ppermute | solution.py:312
  49.5 19.5 %collective-permute-start.39 = (f32[3,16,1024]{2,1,0:T(8,128)S(1)}, f32[3,16,1024]{2,1,0:T(8,128)S(1)}, u32[]{:S(2)}, u32[]{:S(2)}) collective-permute-start(f32[3,16,1024]{2,1,0:T(8,128)S(1)} %get-tuple-element.152), channel_id=1, source_target_pairs={{0,8},{4,12},{8,0},{12,4},{16,24},{20,28},{24,16},{28,20},{1,9},{5... | collective-permute-start | bytes 589832 | tf_op jit(solution)/shard_map/cond/branch_1_fun/ppermute | solution.py:312
  51.1 18.5 %collective-permute-start.40 = (f32[3,16,1024]{2,1,0:T(8,128)S(1)}, f32[3,16,1024]{2,1,0:T(8,128)S(1)}, u32[]{:S(2)}, u32[]{:S(2)}) collective-permute-start(f32[3,16,1024]{2,1,0:T(8,128)S(1)} %get-tuple-element.153), channel_id=1, source_target_pairs={{0,12},{4,8},{8,4},{12,0},{16,28},{20,24},{24,20},{28,16},{1,13},{... | collective-permute-start | bytes 589832 | tf_op jit(solution)/shard_map/cond/branch_1_fun/ppermute | solution.py:312
  65.3 10.1 %collective-permute-start.34 = (f32[3,16,1024]{2,1,0:T(8,128)S(1)}, f32[3,16,1024]{2,1,0:T(8,128)S(1)}, u32[]{:S(2)}, u32[]{:S(2)}) collective-permute-start(f32[3,16,1024]{2,1,0:T(8,128)S(1)} %get-tuple-element.146), channel_id=1, source_target_pairs={{0,4},{4,0},{8,12},{12,8},{16,20},{20,16},{24,28},{28,24},{1,5},{5... | collective-permute-start | bytes 589832 | tf_op jit(solution)/shard_map/cond/branch_1_fun/ppermute | solution.py:312
  67.4 8.0 %collective-permute-start.35 = (f32[3,16,1024]{2,1,0:T(8,128)S(1)}, f32[3,16,1024]{2,1,0:T(8,128)S(1)}, u32[]{:S(2)}, u32[]{:S(2)}) collective-permute-start(f32[3,16,1024]{2,1,0:T(8,128)S(1)} %get-tuple-element.147), channel_id=1, source_target_pairs={{0,8},{4,12},{8,0},{12,4},{16,24},{20,28},{24,16},{28,20},{1,9},{5... | collective-permute-start | bytes 589832 | tf_op jit(solution)/shard_map/cond/branch_1_fun/ppermute | solution.py:312
  67.5 10.0 %collective-permute-start.36 = (f32[3,16,1024]{2,1,0:T(8,128)S(1)}, f32[3,16,1024]{2,1,0:T(8,128)S(1)}, u32[]{:S(2)}, u32[]{:S(2)}) collective-permute-start(f32[3,16,1024]{2,1,0:T(8,128)S(1)} %get-tuple-element.148), channel_id=1, source_target_pairs={{0,12},{4,8},{8,4},{12,0},{16,28},{20,24},{24,20},{28,16},{1,13},{... | collective-permute-start | bytes 589832 | tf_op jit(solution)/shard_map/cond/branch_1_fun/ppermute | solution.py:312
  69.0 6.5 %collective-permute-start.41 = (f32[1,128]{1,0:T(1,128)S(1)}, f32[1,128]{1,0:T(1,128)S(1)}, u32[]{:S(2)}, u32[]{:S(2)}) collective-permute-start(f32[1,128]{1,0:T(1,128)S(1)} %add.45.refs_5_), channel_id=1, source_target_pairs={{0,16},{4,20},{8,24},{12,28},{16,0},{20,4},{24,8},{28,12},{1,17},{... | collective-permute-start | bytes 1544 | tf_op jit(solution)/shard_map/cond/branch_1_fun/ppermute | solution.py:312
  (2 other events, 5.2 us)
